TPU v7x, 32 devices: a whole 2x2x4 slice. The times are simulated.
32 devices in a mesh: row: 4 (over x, core), col: 8 (over z, y).
Axes of the slice: x: 2, y: 2, z: 4, core: 2. Of those that a mesh axis runs over, the one named last changes fastest.
Arguments:
- vectors: float32 [512, 4096], P('row', 'col'), may hold values from -6 to 6
- factors: float32 [8, 4, 512, 512], P('col', None, 'row'), may hold values from -1 to 1, as said below
- offsets: int32 [8], replicated, may hold values from 0 to 1
Outputs:
- updated: float32 [512, 4096], P('row', 'col')
Inputs may be any that keep to these rules, and one draw needn't show every extreme that they name: Each factors[c, k] is an orthogonal matrix.
All inputs are finite; a program needn't handle non-finite values.
Results may differ from a plain program's by a relative error of at most 0.00014.
Values sent between devices are 32-bit elements; how exact they have to be, the bound alone decides.
No kernel may reach another device: no remote copies, remote signals or barrier semaphores. Data moves between devices by JAX's collectives and lax.ppermute only.
A program may use at most 64 MiB of HBM per device.

v0:
```python
import jax
import jax.numpy as jnp
from jax import lax
from jax.sharding import PartitionSpec as P


def passed_along(block, axis, distance):
    devices = range(lax.axis_size(axis))
    route = [(i - distance, i) for i in devices if i - distance in devices]
    return lax.ppermute(block, axis, route)


def product(former, latter):
    return jnp.dot(
        former, latter, precision=lax.Precision.HIGHEST, preferred_element_type=jnp.float32
    )


def one_by_one(section, factor_list, stride):
    for factor_no in range(4):
        before = section[:, : factor_no * stride]
        middle = section[:, factor_no * stride : factor_no * stride + 2 * stride]
        beyond = section[:, factor_no * stride + 2 * stride :]
        section = jnp.concatenate([before, product(middle, factor_list[factor_no]), beyond], 1)
    return section


def keep_panel(assembled):
    return assembled


def on_device(vectors, factors, offsets):
    block_cols = vectors.shape[1]
    stride = block_cols // 2
    column = lax.axis_index("col")
    groups = lax.axis_size("col")
    gathered = lax.all_gather(factors, "row", axis=2, tiled=True)
    chain_factors = gathered[0]
    offset = lax.dynamic_index_in_dim(offsets, column, 0, keepdims=False)
    first_col = offset * stride
    identity = jnp.eye(2 * stride, dtype=jnp.float32)
    global_first = column * block_cols + first_col
    factor_list = []
    for factor_no in range(4):
        valid = global_first + factor_no * stride + 2 * stride <= groups * block_cols
        factor_list.append(jnp.where(valid, chain_factors[factor_no], identity))

    def update(assembled):
        section = lax.dynamic_slice_in_dim(assembled, first_col, 5 * stride, 1)
        section = one_by_one(section, factor_list, stride)
        return lax.dynamic_update_slice_in_dim(assembled, section, first_col, 1)

    beside = passed_along(vectors, "col", -1)
    distant = passed_along(vectors, "col", -2)
    assembled = jnp.concatenate([vectors, beside, distant], 1)
    holding = vectors
    changed = assembled
    position = jnp.mod(column, 3)
    leader = column - position
    for tick_num in range(3):
        position = jnp.mod(column - tick_num, 3)
        leader = column - position
        active = leader >= 0
        if tick_num > 0:
            handed = passed_along(changed[:, block_cols:], "col", 1)
            third = passed_along(holding, "col", -2)
            assembled = jnp.concatenate([handed, third], 1)
        changed = lax.cond(active & (position == 0), update, keep_panel, assembled)
        holding = jnp.where(position == 0, changed[:, :block_cols], holding)
    back_near = passed_along(changed[:, block_cols : 2 * block_cols], "col", 1)
    back_far = passed_along(changed[:, 2 * block_cols :], "col", 2)
    chosen = jnp.where(position == 0, holding, jnp.where(position == 1, back_near, back_far))
    return jnp.where(leader >= 0, chosen, holding)


def solution(mesh):
    placed = (P("row", "col"), P("col", None, "row", None), P())
    return jax.shard_map(
        on_device, mesh=mesh, in_specs=placed, out_specs=P("row", "col"), check_vma=False
    )
```

profile of v0, /device:TPU:12, one launch (start us, length us, event | category | flops | bytes accessed | tf_op | source)
XLA Modules:
  0.0 162.3 jit_solution(18137093932071999158)
XLA Ops:
  7.3 2.4 %collective-permute-start = (f32[128,512]{1,0:T(8,128)}, f32[128,512]{1,0:T(8,128)S(1)}, u32[]{:S(2)}, u32[]{:S(2)}) collective-permute-start(f32[128,512]{1,0:T(8,128)} %param.9), channel_id=1, source_target_pairs={{1,0},{2,1},{3,2},{4,3},{5,4},{6,5},{7,6},{9,8},{10,9},{11,10},{12... | collective-permute-start | bytes 786440 | tf_op jit(solution)/shard_map/ppermute | solution.py:10
  9.7 1.9 %collective-permute-start.1 = (f32[128,512]{1,0:T(8,128)}, f32[128,512]{1,0:T(8,128)S(1)}, u32[]{:S(2)}, u32[]{:S(2)}) collective-permute-start(f32[128,512]{1,0:T(8,128)} %param.9), channel_id=1, source_target_pairs={{2,0},{3,1},{4,2},{5,3},{6,4},{7,5},{10,8},{11,9},{12,10},{13,11},... | collective-permute-start | bytes 786440 | tf_op jit(solution)/shard_map/ppermute | solution.py:10
  14.5 4.9 %collective-permute-done = f32[128,512]{1,0:T(8,128)S(1)} collective-permute-done((f32[128,512]{1,0:T(8,128)}, f32[128,512]{1,0:T(8,128)S(1)}, u32[]{:S(2)}, u32[]{:S(2)}) %collective-permute-start) | collective-permute-done | bytes 262176 | tf_op jit(solution)/shard_map/ppermute | solution.py:10
  20.5 24.0 %all-gather.2.cloned.1.call-done = f32[1,4,512,512]{3,2,1,0:T(8,128)} async-done(((f32[1,4,128,512]{3,2,1,0:T(8,128)}), f32[1,4,512,512]{3,2,1,0:T(8,128)}) %all-gather.2.cloned.1.call-update) | async-done | bytes 4194320 | tf_op jit(solution)/shard_map/all_gather | solution.py:37
  44.5 3.7 %convert_select_fusion = (f32[512,512]{1,0:T(8,128)S(1)}, f32[512,512]{1,0:T(8,128)S(1)}, f32[512,512]{1,0:T(8,128)}, f32[512,512]{1,0:T(8,128)S(1)}) fusion(f32[1,4,512,512]{3,2,1,0:T(8,128)} %all-gather.2.cloned.1.call-done, pred[]{:T(512)S(6)} %le.15, pred[]{:T(512)S(6)} %le.14, pred[]{:T(512)S(6)} %le.13, pred[]{:T(512)S(6)} %le.12), kind=kLoop, calls=%fused_computation.69 | loop fusion | flops 1572864 | bytes 8388612 | tf_op jit(solution)/shard_map/jit(_where)/select_n | solution.py:46
  48.2 17.5 %conditional.3 = (f32[128,1536]{1,0:T(8,128)}) conditional(s32[]{:T(128)} %convert_element_type.20, f32[128,1536]{1,0:T(8,128)} %copy-done, (s32[]{:T(128)}, f32[128,1536]{1,0:T(8,128)}, f32[512,512]{1,0:T(8,128)S(1)}, f32[512,512]{1,0:T(8,128)}, f32[512,512]{1,0:T(8,128)S(1)}, /*index=5*/f32[512,512]{1,0:T(8,128)S(1)}) %tuple.38), branch_computations={%region_0.1_spmd, %region_1.2_spmd} | conditional | flops 1611464704 | bytes 13762710 | solution.py:68
  48.2 2.4 %fusion.6 = f32[128,512]{1,0:T(8,128)} fusion(f32[512,512]{1,0:T(8,128)S(1)} %get-tuple-element.55, f32[128,1536]{1,0:T(8,128)} %get-tuple-element.53, s32[]{:T(128)S(6)} %select_n.67), kind=kOutput, calls=%fused_computation.14 | convolution fusion | flops 402653184 | bytes 1572868 | tf_op jit(solution)/shard_map/cond/branch_1_fun/dot_general | solution.py:14
  51.8 2.0 %fusion.4 = f32[128,512]{1,0:T(8,128)S(1)} fusion(f32[512,512]{1,0:T(8,128)} %get-tuple-element.56, f32[128,768]{1,0:T(8,128)S(1)} %constant_dynamic-slice_fusion.1, f32[128,512]{1,0:T(8,128)} %fusion.6), kind=kOutput, calls=%fused_computation.12 | convolution fusion | flops 402718720 | bytes 1966080 | tf_op jit(solution)/shard_map/cond/branch_1_fun/dot_general | solution.py:14
  59.7 1.9 %pad_maximum_fusion = f32[128,1280]{1,0:T(8,128)} fusion(f32[128,512]{1,0:T(8,128)S(1)} %fusion, f32[128,768]{1,0:T(8,128)} %pad_maximum_fusion.1), kind=kLoop, calls=%fused_computation | loop fusion | flops 163840 | bytes 1310720 | tf_op jit(solution)/shard_map/cond/branch_1_fun/concatenate | solution.py:24
  61.6 4.0 %dynamic_update_slice.6 = f32[128,1536]{1,0:T(8,128)} dynamic-update-slice(f32[128,1536]{1,0:T(8,128)} %get-tuple-element.53, f32[128,1280]{1,0:T(8,128)} %pad_maximum_fusion, s32[]{:T(128)} %constant.26.clone, s32[]{:T(128)S(6)} %select_n.67) | dynamic-update-slice | bytes 1310724 | tf_op jit(solution)/shard_map/cond/branch_1_fun/dynamic_update_slice | solution.py:51
  65.7 1.9 %slice.163 = f32[128,1024]{1,0:T(8,128)} slice(f32[128,1536]{1,0:T(8,128)} %get-tuple-element.77), slice={[0:128], [512:1536]} | slice | bytes 1048576 | tf_op jit(solution)/shard_map/slice | solution.py:65
  67.6 1.9 %collective-permute-start.2 = (f32[128,1024]{1,0:T(8,128)}, f32[128,1024]{1,0:T(8,128)}, u32[]{:S(2)}, u32[]{:S(2)}) collective-permute-start(f32[128,1024]{1,0:T(8,128)} %slice.163), channel_id=1, source_target_pairs={{0,1},{1,2},{2,3},{3,4},{4,5},{5,6},{6,7},{8,9},{9,10},{10,11},{11... | collective-permute-start | bytes 1572872 | tf_op jit(solution)/shard_map/ppermute | solution.py:10
  70.5 1.9 %collective-permute-start.3 = (f32[128,512]{1,0:T(8,128)S(1)}, f32[128,512]{1,0:T(8,128)}, u32[]{:S(2)}, u32[]{:S(2)}) collective-permute-start(f32[128,512]{1,0:T(8,128)S(1)} %slice_select_fusion.2), channel_id=1, source_target_pairs={{2,0},{3,1},{4,2},{5,3},{6,4},{7,5},{10,8},{11,9},{12,10},{13,11},... | collective-permute-start | bytes 786440 | tf_op jit(solution)/shard_map/ppermute | solution.py:10
  72.5 11.4 %collective-permute-done.2 = f32[128,1024]{1,0:T(8,128)} collective-permute-done((f32[128,1024]{1,0:T(8,128)}, f32[128,1024]{1,0:T(8,128)}, u32[]{:S(2)}, u32[]{:S(2)}) %collective-permute-start.2) | collective-permute-done | bytes 524320 | tf_op jit(solution)/shard_map/ppermute | solution.py:10
  83.8 1.9 %constant_dynamic-update-slice_fusion.4 = f32[128,1536]{1,0:T(8,128)} fusion(f32[128,1024]{1,0:T(8,128)} %collective-permute-done.2), kind=kLoop, calls=%fused_computation.86 | loop fusion | bytes 1048576
  87.4 1.9 %slice.165 = f32[128,1024]{1,0:T(8,128)} slice(f32[128,1536]{1,0:T(8,128)} %get-tuple-element.78), slice={[0:128], [512:1536]} | slice | bytes 1048576 | tf_op jit(solution)/shard_map/slice | solution.py:65
  89.3 21.0 %collective-permute-start.4 = (f32[128,1024]{1,0:T(8,128)}, f32[128,1024]{1,0:T(8,128)}, u32[]{:S(2)}, u32[]{:S(2)}) collective-permute-start(f32[128,1024]{1,0:T(8,128)} %slice.165), channel_id=1, source_target_pairs={{0,1},{1,2},{2,3},{3,4},{4,5},{5,6},{6,7},{8,9},{9,10},{10,11},{11... | collective-permute-start | bytes 1572872 | tf_op jit(solution)/shard_map/ppermute | solution.py:10
  111.5 1.9 %collective-permute-start.5 = (f32[128,512]{1,0:T(8,128)S(1)}, f32[128,512]{1,0:T(8,128)}, u32[]{:S(2)}, u32[]{:S(2)}) collective-permute-start(f32[128,512]{1,0:T(8,128)S(1)} %slice_select_fusion.1), channel_id=1, source_target_pairs={{2,0},{3,1},{4,2},{5,3},{6,4},{7,5},{10,8},{11,9},{12,10},{13,11},... | collective-permute-start | bytes 786440 | tf_op jit(solution)/shard_map/ppermute | solution.py:10
  113.4 8.3 %collective-permute-done.4 = f32[128,1024]{1,0:T(8,128)} collective-permute-done((f32[128,1024]{1,0:T(8,128)}, f32[128,1024]{1,0:T(8,128)}, u32[]{:S(2)}, u32[]{:S(2)}) %collective-permute-start.4) | collective-permute-done | bytes 524320 | tf_op jit(solution)/shard_map/ppermute | solution.py:10
  121.7 1.9 %constant_dynamic-update-slice_fusion.6 = f32[128,1536]{1,0:T(8,128)} fusion(f32[128,1024]{1,0:T(8,128)} %collective-permute-done.4), kind=kLoop, calls=%fused_computation.88 | loop fusion | bytes 1048576
  126.4 5.3 %collective-permute-start.6 = (f32[128,512]{1,0:T(8,128)S(1)}, f32[128,512]{1,0:T(8,128)S(1)}, u32[]{:S(2)}, u32[]{:S(2)}) collective-permute-start(f32[128,512]{1,0:T(8,128)S(1)} %get-tuple-element.76), channel_id=1, source_target_pairs={{0,1},{1,2},{2,3},{3,4},{4,5},{5,6},{6,7},{8,9},{9,10},{10,11},{11... | collective-permute-start | bytes 786440 | tf_op jit(solution)/shard_map/ppermute | solution.py:10
  131.7 12.7 %collective-permute-start.7 = (f32[128,512]{1,0:T(8,128)S(1)}, f32[128,512]{1,0:T(8,128)S(1)}, u32[]{:S(2)}, u32[]{:S(2)}) collective-permute-start(f32[128,512]{1,0:T(8,128)S(1)} %get-tuple-element.75), channel_id=1, source_target_pairs={{0,2},{1,3},{2,4},{3,5},{4,6},{5,7},{8,10},{9,11},{10,12},{11,13},... | collective-permute-start | bytes 786440 | tf_op jit(solution)/shard_map/ppermute | solution.py:10
  144.3 2.5 %collective-permute-done.6 = f32[128,512]{1,0:T(8,128)S(1)} collective-permute-done((f32[128,512]{1,0:T(8,128)S(1)}, f32[128,512]{1,0:T(8,128)S(1)}, u32[]{:S(2)}, u32[]{:S(2)}) %collective-permute-start.6) | collective-permute-done | bytes 262176 | tf_op jit(solution)/shard_map/ppermute | solution.py:10
  146.8 6.8 %collective-permute-done.7 = f32[128,512]{1,0:T(8,128)S(1)} collective-permute-done((f32[128,512]{1,0:T(8,128)S(1)}, f32[128,512]{1,0:T(8,128)S(1)}, u32[]{:S(2)}, u32[]{:S(2)}) %collective-permute-start.7) | collective-permute-done | bytes 262176 | tf_op jit(solution)/shard_map/ppermute | solution.py:10
  (33 shorter events, 19.4 us)
Async XLA Ops:
  6.5 38.0 %all-gather.2.cloned.1.call-start = ((), (), s32[]{:S(2)}) async-start(), calls=%async_computation | async-start | bytes 5242880 | tf_op jit(solution)/shard_map/all_gather | solution.py:37
  7.3 12.2 %collective-permute-start = (f32[128,512]{1,0:T(8,128)}, f32[128,512]{1,0:T(8,128)S(1)}, u32[]{:S(2)}, u32[]{:S(2)}) collective-permute-start(f32[128,512]{1,0:T(8,128)} %param.9), channel_id=1, source_target_pairs={{1,0},{2,1},{3,2},{4,3},{5,4},{6,5},{7,6},{9,8},{10,9},{11,10},{12... | collective-permute-start | bytes 786440 | tf_op jit(solution)/shard_map/ppermute | solution.py:10
  9.7 9.9 %collective-permute-start.1 = (f32[128,512]{1,0:T(8,128)}, f32[128,512]{1,0:T(8,128)S(1)}, u32[]{:S(2)}, u32[]{:S(2)}) collective-permute-start(f32[128,512]{1,0:T(8,128)} %param.9), channel_id=1, source_target_pairs={{2,0},{3,1},{4,2},{5,3},{6,4},{7,5},{10,8},{11,9},{12,10},{13,11},... | collective-permute-start | bytes 786440 | tf_op jit(solution)/shard_map/ppermute | solution.py:10
  19.6 0.9 copy-start
  50.6 5.7 %slice-start = ((f32[128,512]{1,0:T(8,128)}), f32[128,256]{1,0:T(8,128)S(1)}, s32[]{:S(2)}) async-start(f32[128,512]{1,0:T(8,128)} %fusion.6), calls=%async_computation.1 | async-start | bytes 262144 | tf_op jit(solution)/shard_map/cond/branch_1_fun/slice | solution.py:21
  55.6 0.7 copy-start.1
  67.6 16.3 %collective-permute-start.2 = (f32[128,1024]{1,0:T(8,128)}, f32[128,1024]{1,0:T(8,128)}, u32[]{:S(2)}, u32[]{:S(2)}) collective-permute-start(f32[128,1024]{1,0:T(8,128)} %slice.163), channel_id=1, source_target_pairs={{0,1},{1,2},{2,3},{3,4},{4,5},{5,6},{6,7},{8,9},{9,10},{10,11},{11... | collective-permute-start | bytes 1572872 | tf_op jit(solution)/shard_map/ppermute | solution.py:10
  70.5 17.0 %copy-start.4 = (f32[128,512]{1,0:T(8,128)}, f32[128,512]{1,0:T(8,128)S(1)}, u32[]{:S(2)}) copy-start(f32[128,512]{1,0:T(8,128)S(1)} %slice_select_fusion.2) | copy-start | bytes 786436
  70.5 15.2 %collective-permute-start.3 = (f32[128,512]{1,0:T(8,128)S(1)}, f32[128,512]{1,0:T(8,128)}, u32[]{:S(2)}, u32[]{:S(2)}) collective-permute-start(f32[128,512]{1,0:T(8,128)S(1)} %slice_select_fusion.2), channel_id=1, source_target_pairs={{2,0},{3,1},{4,2},{5,3},{6,4},{7,5},{10,8},{11,9},{12,10},{13,11},... | collective-permute-start | bytes 786440 | tf_op jit(solution)/shard_map/ppermute | solution.py:10
  89.3 32.4 %collective-permute-start.4 = (f32[128,1024]{1,0:T(8,128)}, f32[128,1024]{1,0:T(8,128)}, u32[]{:S(2)}, u32[]{:S(2)}) collective-permute-start(f32[128,1024]{1,0:T(8,128)} %slice.165), channel_id=1, source_target_pairs={{0,1},{1,2},{2,3},{3,4},{4,5},{5,6},{6,7},{8,9},{9,10},{10,11},{11... | collective-permute-start | bytes 1572872 | tf_op jit(solution)/shard_map/ppermute | solution.py:10
  111.5 13.8 %copy-start.3 = (f32[128,512]{1,0:T(8,128)}, f32[128,512]{1,0:T(8,128)S(1)}, u32[]{:S(2)}) copy-start(f32[128,512]{1,0:T(8,128)S(1)} %slice_select_fusion.1) | copy-start | bytes 786436
  111.5 12.1 %collective-permute-start.5 = (f32[128,512]{1,0:T(8,128)S(1)}, f32[128,512]{1,0:T(8,128)}, u32[]{:S(2)}, u32[]{:S(2)}) collective-permute-start(f32[128,512]{1,0:T(8,128)S(1)} %slice_select_fusion.1), channel_id=1, source_target_pairs={{2,0},{3,1},{4,2},{5,3},{6,4},{7,5},{10,8},{11,9},{12,10},{13,11},... | collective-permute-start | bytes 786440 | tf_op jit(solution)/shard_map/ppermute | solution.py:10
  126.4 20.5 %collective-permute-start.6 = (f32[128,512]{1,0:T(8,128)S(1)}, f32[128,512]{1,0:T(8,128)S(1)}, u32[]{:S(2)}, u32[]{:S(2)}) collective-permute-start(f32[128,512]{1,0:T(8,128)S(1)} %get-tuple-element.76), channel_id=1, source_target_pairs={{0,1},{1,2},{2,3},{3,4},{4,5},{5,6},{6,7},{8,9},{9,10},{10,11},{11... | collective-permute-start | bytes 786440 | tf_op jit(solution)/shard_map/ppermute | solution.py:10
  131.7 22.0 %collective-permute-start.7 = (f32[128,512]{1,0:T(8,128)S(1)}, f32[128,512]{1,0:T(8,128)S(1)}, u32[]{:S(2)}, u32[]{:S(2)}) collective-permute-start(f32[128,512]{1,0:T(8,128)S(1)} %get-tuple-element.75), channel_id=1, source_target_pairs={{0,2},{1,3},{2,4},{3,5},{4,6},{5,7},{8,10},{9,11},{10,12},{11,13},... | collective-permute-start | bytes 786440 | tf_op jit(solution)/shard_map/ppermute | solution.py:10
Sparse Core Ops, SparseCore 0:
  8.9 35.5 all-gather.1
where the time goes:
time: 163 us; the launch traced here: 162 us
  waiting for transfers between devices  58.7 us (36%)
  starting transfers between devices  49.1 us (30%)
  local copies, waits for them, and re-layouts  23.2 us (14%)
  between operations  14.3 us (9%)
  other arithmetic  10.3 us (6%)
  matrix products  6.76 us (4%)
    ppermute x8, starting transfers between devices, passed_along(): return lax.ppermute(block, axis, route)  49.1 us
    ppermute x8, waiting for transfers between devices, passed_along(): return lax.ppermute(block, axis, route)  34 us
    all_gather x1, waiting for transfers between devices, on_device(): gathered = lax.all_gather(factors, 'row', axis=2, tiled=True)  24 us
    dot_general x4, matrix products, product(): jnp.dot(former, latter, precision=lax.Precision.HIGHEST, preferred_elemen...  6.76 us
    unnamed x10, local copies, waits for them, and re-layouts  5.69 us
    dynamic_update_slice x1, local copies, waits for them, and re-layouts, update(): return lax.dynamic_update_slice_in_dim(assembled, section, first_col, 1)  4.03 us
    slice x2, local copies, waits for them, and re-layouts, on_device(): handed = passed_along(changed[:, block_cols:], 'col', 1)  3.79 us
    select_n x1, other arithmetic, on_device(): factor_list.append(jnp.where(valid, chain_factors[factor_no], identity))  3.68 us
  transfers between devices with their start and end apart: 9, of which 7 were waited for; matrix products, arithmetic and copies ran while one was open for 5% of the time, Pallas kernels for 0%

commit v1 on v0

v1 whole, which is shorter than its diff:
```python
import functools

import jax
import jax.numpy as jnp
from jax import lax
from jax.experimental import pallas as pl
from jax.experimental.pallas import tpu as pltpu
from jax.sharding import PartitionSpec as P


FACTORS = 4
TICKS = 3


def split_halves(value):
    high = value.astype(jnp.bfloat16)
    low = (value - high.astype(jnp.float32)).astype(jnp.bfloat16)
    return high, low


def product(former, high_ref, low_ref):
    rows = former.shape[0]
    high, low = split_halves(former)
    both = jnp.concatenate([high, low], 0)
    first = jnp.dot(both, high_ref[...], preferred_element_type=jnp.float32)
    second = jnp.dot(high, low_ref[...], preferred_element_type=jnp.float32)
    return first[:rows] + (first[rows:] + second)


def place(groups, offsets_ref):
    column = lax.axis_index("col")
    offset = offsets_ref[column]
    last = 2 * groups - 2 - 2 * column - offset
    return column, lax.rem(column, TICKS), offset, last


def convert(pieces, high_ref, low_ref):
    height = pieces[0].shape[0]
    row = lax.axis_index("row")
    for mask, piece in enumerate(pieces):
        high, low = split_halves(piece[...])
        start = pl.multiple_of((row ^ mask) * height, height)
        high_ref[pl.ds(start, height), :] = high
        low_ref[pl.ds(start, height), :] = low


def strips(first, count, stride):
    return (slice(None), pl.ds(pl.multiple_of(first * stride, stride), count * stride))


def early_kernel(groups, ring, numbers, stride, *refs):
    count = len(numbers)
    refs = list(refs)
    offsets_ref = refs.pop(0)
    shift = numbers[0]
    blocks = [refs.pop(0) for _ in range(3 if shift == 0 else 1)]
    pieces = [refs.pop(0) for _ in range(count * ring)]
    results = [refs.pop(0) for _ in range(1 if numbers[-1] == FACTORS - 1 else 2)]
    kept = [refs.pop(0) for _ in range(2 * count)]
    (buf,) = refs
    _, tick, offset, last = place(groups, offsets_ref)
    active = tick == 0

    @pl.when(active)
    def _():
        width = blocks[0].shape[1]
        for i, block in enumerate(blocks):
            buf[:, i * width : (i + 1) * width] = block[...]

    for i, number in enumerate(numbers):
        convert(pieces[i * ring : (i + 1) * ring], kept[2 * i], kept[2 * i + 1])

        @pl.when(active & (number <= last))
        def _():
            begin = 0 if shift == 3 else offset + number - shift
            here = strips(begin, 2, stride)
            buf[here] = product(buf[here], kept[2 * i], kept[2 * i + 1])

    @pl.when(active)
    def _():
        if shift == 0:
            results[0][...] = buf[:, : 2 * stride]
            results[1][...] = buf[:, 2 * stride :]
        elif shift == 2:
            results[0][:, :stride] = buf[:, :stride]
            results[0][:, stride:] = buf[strips(3 - 2 * offset, 1, stride)]
            results[1][...] = buf[strips(1 + offset, 2, stride)]
        else:
            results[0][...] = buf[...]


def late_kernel(groups, when, stride, *refs):
    offsets_ref, outer, final, third = refs[:4]
    weights = refs[4 : 4 + 2 * FACTORS]
    results = refs[4 + 2 * FACTORS : 7 + 2 * FACTORS]
    (buf,) = refs[7 + 2 * FACTORS :]
    column, tick, offset, last = place(groups, offsets_ref)
    before = offsets_ref[jnp.maximum(column - 1, 0)]

    @pl.when(tick == when)
    def _():
        buf[:, :stride] = outer[:, :stride]
        buf[strips(3 - 2 * before, 1, stride)] = outer[:, stride:]
        buf[strips(1 + before, 2, stride)] = final[...]
        buf[:, 4 * stride :] = third[...]
        for number in range(FACTORS):

            @pl.when(number <= last)
            def _():
                here = strips(offset + number, 2, stride)
                buf[here] = product(buf[here], weights[2 * number], weights[2 * number + 1])

        results[0][...] = buf[:, : 2 * stride]
        if when == TICKS - 1:
            results[1][...] = buf[:, 2 * stride : 4 * stride]
            results[2][...] = buf[:, 4 * stride :]
        else:
            results[1][:, :stride] = buf[:, 2 * stride : 3 * stride]
            results[1][:, stride:] = buf[strips(5 - 2 * offset, 1, stride)]
            results[2][...] = buf[strips(3 + offset, 2, stride)]


def pick_kernel(own0, own1, own2, near, far, out):
    column = lax.axis_index("col")
    tick = lax.rem(column, TICKS)
    for source, chosen in (
        (own0, (tick == 0) & (column < TICKS)),
        (near, (tick == 0) & (column >= TICKS)),
        (own1, (tick == 1) & (column < TICKS)),
        (far, (tick == 1) & (column >= TICKS)),
        (own2, tick == 2),
    ):

        @pl.when(chosen)
        def _():
            out[...] = source[...]


def on_device(groups, ring, vectors, factors, offsets):
    rows, width = vectors.shape
    stride = width // 2
    height = factors.shape[2]
    order = ring * height
    f32, bf16 = jnp.float32, jnp.bfloat16
    on_chip = pl.BlockSpec(memory_space=pltpu.VMEM)
    scalars = pl.BlockSpec(memory_space=pltpu.SMEM)
    bits = [1 << i for i in range(ring.bit_length() - 1)][::-1]

    def along(array, distance, tick):
        pairs = [
            (i, i + distance)
            for i in range(groups)
            if i % TICKS == tick and 0 <= i + distance < groups
        ]
        return lax.ppermute(array, "col", pairs)

    def swapped(array, bit):
        return lax.ppermute(array, "row", [(i, i ^ bit) for i in range(ring)])

    def call(kernel, outs, scratch, *operands):
        return pl.pallas_call(
            kernel,
            out_shape=outs,
            in_specs=[scalars if op.dtype == jnp.int32 else on_chip for op in operands],
            out_specs=[on_chip] * len(outs),
            scratch_shapes=scratch,
            compiler_params=pltpu.CompilerParams(vmem_limit_bytes=24 << 20),
        )(*operands)

    def block(columns=width, dtype=f32, high=rows):
        return jax.ShapeDtypeStruct((high, columns), dtype)

    gathered = []
    for number in range(FACTORS):
        pieces = {0: factors[0, number]}
        for bit in bits:
            for mask in list(pieces):
                pieces[mask ^ bit] = swapped(pieces[mask], bit)
        gathered.append([pieces[mask] for mask in range(ring)])

    beside = along(vectors, -1, 1)
    distant = along(vectors, -2, 2)

    def early(numbers, blocks, outs):
        count = len(numbers)
        kept = [block(order, bf16, order)] * (2 * count)
        span = sum(b.shape[1] for b in blocks)
        scratch = [pltpu.VMEM((rows, span), f32)]
        pieces = [piece for number in numbers for piece in gathered[number]]
        results = call(
            functools.partial(early_kernel, groups, ring, numbers, stride),
            outs + kept,
            scratch,
            offsets,
            *blocks,
            *pieces,
        )
        return results[: len(outs)], results[len(outs) :]

    (own0, rest), kept01 = early((0, 1), [vectors, beside, distant], [block(), block(2 * width)])
    third = along(own0, -2, 0)
    (outer, passing), kept2 = early((2,), [rest], [block(), block()])
    outer = along(outer, 1, 0)
    (final,), kept3 = early((3,), [passing], [block()])
    final = along(final, 1, 0)
    weights = [*kept01, *kept2, *kept3]

    def late(when, outer, final, third):
        scratch = [pltpu.VMEM((rows, 3 * width), f32)]
        return call(
            functools.partial(late_kernel, groups, when, stride),
            [block()] * 3,
            scratch,
            offsets,
            outer,
            final,
            third,
            *weights,
        )

    own1, outer, final = late(1, outer, final, third)
    third = along(own1, -2, 1)
    outer = along(outer, 1, 1)
    final = along(final, 1, 1)
    own2, near, far = late(2, outer, final, third)
    near = along(near, 1, 2)
    far = along(far, 2, 2)
    (out,) = call(pick_kernel, [block()], [], own0, own1, own2, near, far)
    return out


def solution(mesh):
    placed = (P("row", "col"), P("col", None, "row", None), P())
    body = functools.partial(on_device, mesh.shape["col"], mesh.shape["row"])
    return jax.shard_map(
        body, mesh=mesh, in_specs=placed, out_specs=P("row", "col"), check_vma=False
    )
```

time: 163 us -> 78.2 us (0.48)
  the two profiles are of different devices: /device:TPU:12 before, /device:TPU:28 now
where the time goes in v1:
time: 78.2 us; the launch traced here: 77.9 us
  waiting for transfers between devices  55.1 us (70%)
  starting transfers between devices  16.7 us (21%)
  Pallas kernels  4.69 us (6%)
  local copies, waits for them, and re-layouts  1.31 us (2%)
    ppermute x10, waiting for transfers between devices, along(): return lax.ppermute(array, 'col', pairs)  36.8 us
    ppermute x12, waiting for transfers between devices, swapped(): return lax.ppermute(array, 'row', [(i, i ^ bit) for i in range(ring)])  18.2 us
    ppermute x10, starting transfers between devices, along(): return lax.ppermute(array, 'col', pairs)  11 us
    ppermute x12, starting transfers between devices, swapped(): return lax.ppermute(array, 'row', [(i, i ^ bit) for i in range(ring)])  5.72 us
    pallas_call x6, Pallas kernels, call(): pl.pallas_call(kernel, out_shape=outs, in_specs=[scalars if op.dtype == j...  4.69 us
  transfers between devices with their start and end apart: 22, of which 8 were waited for; matrix products, arithmetic and copies ran while one was open for 0% of the time, Pallas kernels for 2%

profile of v1, /device:TPU:28, one launch (start us, length us, event | category | flops | bytes accessed | tf_op | source)
XLA Modules:
  0.0 77.9 jit_solution(8544222489392292340)
XLA Ops:
  0.0 1.3 %slice_bitcast_fusion = (f32[128,512]{1,0:T(8,128)S(1)}, f32[128,512]{1,0:T(8,128)S(1)}, f32[128,512]{1,0:T(8,128)S(1)}, f32[128,512]{1,0:T(8,128)S(1)}) fusion(f32[1,4,128,512]{3,2,1,0:T(8,128)} %param.4), kind=kLoop, calls=%fused_computation | loop fusion | bytes 2097152 | tf_op jit(solution)/shard_map/squeeze | solution.py:175
  1.3 1.6 %collective-permute-start.3 = (f32[128,512]{1,0:T(8,128)S(1)}, f32[128,512]{1,0:T(8,128)S(1)}, u32[]{:S(2)}, u32[]{:S(2)}) collective-permute-start(f32[128,512]{1,0:T(8,128)S(1)} %get-tuple-element.45.refs_4_), channel_id=1, source_target_pairs={{0,16},{8,24},{16,0},{24,8},{1,17},{9,25},{17,1},{25,9},{2,18},{10... | collective-permute-start | bytes 786440 | tf_op jit(solution)/shard_map/ppermute | solution.py:158
  3.9 2.4 %collective-permute-start = (f32[128,512]{1,0:T(8,128)S(1)}, f32[128,512]{1,0:T(8,128)S(1)}, u32[]{:S(2)}, u32[]{:S(2)}) collective-permute-start(f32[128,512]{1,0:T(8,128)S(1)} %copy-done), channel_id=1, source_target_pairs={{1,0},{4,3},{7,6},{9,8},{12,11},{15,14},{17,16},{20,19},{23,22},{2... | collective-permute-start | bytes 786440 | tf_op jit(solution)/shard_map/ppermute | solution.py:155
  6.3 4.2 %collective-permute-done.3.refs_6_ = f32[128,512]{1,0:T(8,128)S(1)} collective-permute-done((f32[128,512]{1,0:T(8,128)S(1)}, f32[128,512]{1,0:T(8,128)S(1)}, u32[]{:S(2)}, u32[]{:S(2)}) %collective-permute-start.3) | collective-permute-done | bytes 262176 | tf_op jit(solution)/shard_map/ppermute | solution.py:158
  11.2 3.8 %collective-permute-done.6.refs_10_ = f32[128,512]{1,0:T(8,128)S(1)} collective-permute-done((f32[128,512]{1,0:T(8,128)S(1)}, f32[128,512]{1,0:T(8,128)S(1)}, u32[]{:S(2)}, u32[]{:S(2)}) %collective-permute-start.6) | collective-permute-done | bytes 262176 | tf_op jit(solution)/shard_map/ppermute | solution.py:158
  15.0 1.5 %collective-permute-start.9 = (f32[128,512]{1,0:T(8,128)S(1)}, f32[128,512]{1,0:T(8,128)S(1)}, u32[]{:S(2)}, u32[]{:S(2)}) collective-permute-start(f32[128,512]{1,0:T(8,128)S(1)} %get-tuple-element.46.refs_2_), channel_id=1, source_target_pairs={{0,16},{8,24},{16,0},{24,8},{1,17},{9,25},{17,1},{25,9},{2,18},{10... | collective-permute-start | bytes 786440 | tf_op jit(solution)/shard_map/ppermute | solution.py:158
  17.7 6.6 %collective-permute-done.9.refs_4_ = f32[128,512]{1,0:T(8,128)S(1)} collective-permute-done((f32[128,512]{1,0:T(8,128)S(1)}, f32[128,512]{1,0:T(8,128)S(1)}, u32[]{:S(2)}, u32[]{:S(2)}) %collective-permute-start.9) | collective-permute-done | bytes 262176 | tf_op jit(solution)/shard_map/ppermute | solution.py:158
  24.2 3.6 %collective-permute-done.13.refs_4_ = f32[128,512]{1,0:T(8,128)S(1)} collective-permute-done((f32[128,512]{1,0:T(8,128)S(1)}, f32[128,512]{1,0:T(8,128)S(1)}, u32[]{:S(2)}, u32[]{:S(2)}) %collective-permute-start.13) | collective-permute-done | bytes 262176 | tf_op jit(solution)/shard_map/ppermute | solution.py:158
  28.4 0.9 %shard_map.37 = (f32[128,512]{1,0:T(8,128)S(1)}, f32[128,1024]{1,0:T(8,128)S(1)}, bf16[512,512]{1,0:T(8,128)(2,1)S(1)}, bf16[512,512]{1,0:T(8,128)(2,1)S(1)}, bf...) custom-call(s32[8]{0:T(128)S(1)} %copy-done.1, f32[128,512]{1,0:T(8,128)S(1)} %copy-done, ...), custom_call_target="tpu_custom_call" | custom-call | tf_op jit(solution)/shard_map/pallas_call | solution.py:161
  29.3 0.7 shard_map.38
  30.1 0.7 shard_map.39
  30.8 1.3 %collective-permute-start.15 = (f32[128,512]{1,0:T(8,128)S(1)}, f32[128,512]{1,0:T(8,128)S(1)}, u32[]{:S(2)}, u32[]{:S(2)}) collective-permute-start(f32[128,512]{1,0:T(8,128)S(1)} %get-tuple-element.28), channel_id=1, source_target_pairs={{0,1},{3,4},{6,7},{8,9},{11,12},{14,15},{16,17},{19,20},{22,23},{2... | collective-permute-start | bytes 786440 | tf_op jit(solution)/shard_map/ppermute | solution.py:155
  32.1 1.3 %collective-permute-start.11 = (f32[128,512]{1,0:T(8,128)S(1)}, f32[128,512]{1,0:T(8,128)S(1)}, u32[]{:S(2)}, u32[]{:S(2)}) collective-permute-start(f32[128,512]{1,0:T(8,128)S(1)} %get-tuple-element.26), channel_id=1, source_target_pairs={{0,1},{3,4},{6,7},{8,9},{11,12},{14,15},{16,17},{19,20},{22,23},{2... | collective-permute-start | bytes 786440 | tf_op jit(solution)/shard_map/ppermute | solution.py:155
  33.4 0.7 collective-permute-start.16
  34.1 7.8 %collective-permute-done.15.refs_2_ = f32[128,512]{1,0:T(8,128)S(1)} collective-permute-done((f32[128,512]{1,0:T(8,128)S(1)}, f32[128,512]{1,0:T(8,128)S(1)}, u32[]{:S(2)}, u32[]{:S(2)}) %collective-permute-start.15) | collective-permute-done | bytes 262176 | tf_op jit(solution)/shard_map/ppermute | solution.py:155
  41.9 4.7 %collective-permute-done.11.refs_1_ = f32[128,512]{1,0:T(8,128)S(1)} collective-permute-done((f32[128,512]{1,0:T(8,128)S(1)}, f32[128,512]{1,0:T(8,128)S(1)}, u32[]{:S(2)}, u32[]{:S(2)}) %collective-permute-start.11) | collective-permute-done | bytes 262176 | tf_op jit(solution)/shard_map/ppermute | solution.py:155
  46.5 1.0 %shard_map.40 = (f32[128,512]{1,0:T(8,128)S(1)}, f32[128,512]{1,0:T(8,128)S(1)}, f32[128,512]{1,0:T(8,128)S(1)}) custom-call(s32[8]{0:T(128)S(1)} %copy-done.1, f32[128,512]{1,0:T(8,128)S(1)} %collective-permute-done.11.refs_1_, f32[128,512]{1,0:T(8,128)S(1)} %collective-permute-done.15.refs_2_, f32[128,512]{1,0:T(8,128)S(1)} %collective-permute-done.16.refs_3_, ...), custom_call_target="tpu_custom_call" | custom-call | tf_op jit(solution)/shard_map/pallas_call | solution.py:161
  47.6 0.7 collective-permute-start.17
  48.3 0.7 collective-permute-start.18
  49.0 1.3 %collective-permute-start.19 = (f32[128,512]{1,0:T(8,128)S(1)}, f32[128,512]{1,0:T(8,128)S(1)}, u32[]{:S(2)}, u32[]{:S(2)}) collective-permute-start(f32[128,512]{1,0:T(8,128)S(1)} %get-tuple-element.37.own1), channel_id=1, source_target_pairs={{4,2},{7,5},{12,10},{15,13},{20,18},{23,21},{28,26},{31,29}} | collective-permute-start | bytes 786440 | tf_op jit(solution)/shard_map/ppermute | solution.py:155
  50.3 5.1 %collective-permute-done.19.refs_3_ = f32[128,512]{1,0:T(8,128)S(1)} collective-permute-done((f32[128,512]{1,0:T(8,128)S(1)}, f32[128,512]{1,0:T(8,128)S(1)}, u32[]{:S(2)}, u32[]{:S(2)}) %collective-permute-start.19) | collective-permute-done | bytes 262176 | tf_op jit(solution)/shard_map/ppermute | solution.py:155
  56.7 1.3 %collective-permute-start.21 = (f32[128,512]{1,0:T(8,128)S(1)}, f32[128,512]{1,0:T(8,128)S(1)}, u32[]{:S(2)}, u32[]{:S(2)}) collective-permute-start(f32[128,512]{1,0:T(8,128)S(1)} %get-tuple-element.42), channel_id=1, source_target_pairs={{2,4},{5,7},{10,12},{13,15},{18,20},{21,23},{26,28},{29,31}} | collective-permute-start | bytes 786440 | tf_op jit(solution)/shard_map/ppermute | solution.py:155
  58.0 19.2 %collective-permute-done.21.far = f32[128,512]{1,0:T(8,128)S(1)} collective-permute-done((f32[128,512]{1,0:T(8,128)S(1)}, f32[128,512]{1,0:T(8,128)S(1)}, u32[]{:S(2)}, u32[]{:S(2)}) %collective-permute-start.21) | collective-permute-done | bytes 262176 | tf_op jit(solution)/shard_map/ppermute | solution.py:155
  77.2 0.7 shard_map.42
  (31 shorter events, 4.6 us)
Async XLA Ops:
  0.0 3.9 %copy-start = (f32[128,512]{1,0:T(8,128)S(1)}, f32[128,512]{1,0:T(8,128)}, u32[]{:S(2)}) copy-start(f32[128,512]{1,0:T(8,128)} %refs_1_.1) | copy-start | bytes 786436
  1.3 9.2 %collective-permute-start.3 = (f32[128,512]{1,0:T(8,128)S(1)}, f32[128,512]{1,0:T(8,128)S(1)}, u32[]{:S(2)}, u32[]{:S(2)}) collective-permute-start(f32[128,512]{1,0:T(8,128)S(1)} %get-tuple-element.45.refs_4_), channel_id=1, source_target_pairs={{0,16},{8,24},{16,0},{24,8},{1,17},{9,25},{17,1},{25,9},{2,18},{10... | collective-permute-start | bytes 786440 | tf_op jit(solution)/shard_map/ppermute | solution.py:158
  2.9 12.2 %collective-permute-start.6 = (f32[128,512]{1,0:T(8,128)S(1)}, f32[128,512]{1,0:T(8,128)S(1)}, u32[]{:S(2)}, u32[]{:S(2)}) collective-permute-start(f32[128,512]{1,0:T(8,128)S(1)} %get-tuple-element.44.refs_8_), channel_id=1, source_target_pairs={{0,16},{8,24},{16,0},{24,8},{1,17},{9,25},{17,1},{25,9},{2,18},{10... | collective-permute-start | bytes 786440 | tf_op jit(solution)/shard_map/ppermute | solution.py:158
  3.4 13.1 %collective-permute-start.2 = (f32[128,512]{1,0:T(8,128)S(1)}, f32[128,512]{1,0:T(8,128)S(1)}, u32[]{:S(2)}, u32[]{:S(2)}) collective-permute-start(f32[128,512]{1,0:T(8,128)S(1)} %get-tuple-element.45.refs_4_), channel_id=1, source_target_pairs={{0,8},{8,0},{16,24},{24,16},{1,9},{9,1},{17,25},{25,17},{2,10},{10... | collective-permute-start | bytes 786440 | tf_op jit(solution)/shard_map/ppermute | solution.py:158
  3.4 13.7 %collective-permute-start.5 = (f32[128,512]{1,0:T(8,128)S(1)}, f32[128,512]{1,0:T(8,128)S(1)}, u32[]{:S(2)}, u32[]{:S(2)}) collective-permute-start(f32[128,512]{1,0:T(8,128)S(1)} %get-tuple-element.44.refs_8_), channel_id=1, source_target_pairs={{0,8},{8,0},{16,24},{24,16},{1,9},{9,1},{17,25},{25,17},{2,10},{10... | collective-permute-start | bytes 786440 | tf_op jit(solution)/shard_map/ppermute | solution.py:158
  3.9 13.2 %collective-permute-start = (f32[128,512]{1,0:T(8,128)S(1)}, f32[128,512]{1,0:T(8,128)S(1)}, u32[]{:S(2)}, u32[]{:S(2)}) collective-permute-start(f32[128,512]{1,0:T(8,128)S(1)} %copy-done), channel_id=1, source_target_pairs={{1,0},{4,3},{7,6},{9,8},{12,11},{15,14},{17,16},{20,19},{23,22},{2... | collective-permute-start | bytes 786440 | tf_op jit(solution)/shard_map/ppermute | solution.py:155
  10.6 7.0 %collective-permute-start.1 = (f32[128,512]{1,0:T(8,128)S(1)}, f32[128,512]{1,0:T(8,128)S(1)}, u32[]{:S(2)}, u32[]{:S(2)}) collective-permute-start(f32[128,512]{1,0:T(8,128)S(1)} %copy-done), channel_id=1, source_target_pairs={{2,0},{5,3},{10,8},{13,11},{18,16},{21,19},{26,24},{29,27}} | collective-permute-start | bytes 786440 | tf_op jit(solution)/shard_map/ppermute | solution.py:155
  15.0 13.3 %copy-start.1 = (s32[8]{0:T(128)S(1)}, s32[8]{0:T(128)}, u32[]{:S(2)}) copy-start(s32[8]{0:T(128)} %refs_0_.9) | copy-start | bytes 100
  15.0 9.2 %collective-permute-start.9 = (f32[128,512]{1,0:T(8,128)S(1)}, f32[128,512]{1,0:T(8,128)S(1)}, u32[]{:S(2)}, u32[]{:S(2)}) collective-permute-start(f32[128,512]{1,0:T(8,128)S(1)} %get-tuple-element.46.refs_2_), channel_id=1, source_target_pairs={{0,16},{8,24},{16,0},{24,8},{1,17},{9,25},{17,1},{25,9},{2,18},{10... | collective-permute-start | bytes 786440 | tf_op jit(solution)/shard_map/ppermute | solution.py:158
  16.5 11.3 %collective-permute-start.13 = (f32[128,512]{1,0:T(8,128)S(1)}, f32[128,512]{1,0:T(8,128)S(1)}, u32[]{:S(2)}, u32[]{:S(2)}) collective-permute-start(f32[128,512]{1,0:T(8,128)S(1)} %get-tuple-element.43.refs_2_), channel_id=1, source_target_pairs={{0,16},{8,24},{16,0},{24,8},{1,17},{9,25},{17,1},{25,9},{2,18},{10... | collective-permute-start | bytes 786440 | tf_op jit(solution)/shard_map/ppermute | solution.py:158
  17.1 10.8 %collective-permute-start.4 = (f32[128,512]{1,0:T(8,128)S(1)}, f32[128,512]{1,0:T(8,128)S(1)}, u32[]{:S(2)}, u32[]{:S(2)}) collective-permute-start(f32[128,512]{1,0:T(8,128)S(1)} %collective-permute-done.3.refs_6_), channel_id=1, source_target_pairs={{0,8},{8,0},{16,24},{24,16},{1,9},{9,1},{17,25},{25,17},{2,10},{10... | collective-permute-start | bytes 786440 | tf_op jit(solution)/shard_map/ppermute | solution.py:158
  17.1 11.3 %collective-permute-start.7 = (f32[128,512]{1,0:T(8,128)S(1)}, f32[128,512]{1,0:T(8,128)S(1)}, u32[]{:S(2)}, u32[]{:S(2)}) collective-permute-start(f32[128,512]{1,0:T(8,128)S(1)} %collective-permute-done.6.refs_10_), channel_id=1, source_target_pairs={{0,8},{8,0},{16,24},{24,16},{1,9},{9,1},{17,25},{25,17},{2,10},{10... | collective-permute-start | bytes 786440 | tf_op jit(solution)/shard_map/ppermute | solution.py:158
  17.6 11.7 %collective-permute-start.8 = (f32[128,512]{1,0:T(8,128)S(1)}, f32[128,512]{1,0:T(8,128)S(1)}, u32[]{:S(2)}, u32[]{:S(2)}) collective-permute-start(f32[128,512]{1,0:T(8,128)S(1)} %get-tuple-element.46.refs_2_), channel_id=1, source_target_pairs={{0,8},{8,0},{16,24},{24,16},{1,9},{9,1},{17,25},{25,17},{2,10},{10... | collective-permute-start | bytes 786440 | tf_op jit(solution)/shard_map/ppermute | solution.py:158
  24.2 5.1 %collective-permute-start.10 = (f32[128,512]{1,0:T(8,128)S(1)}, f32[128,512]{1,0:T(8,128)S(1)}, u32[]{:S(2)}, u32[]{:S(2)}) collective-permute-start(f32[128,512]{1,0:T(8,128)S(1)} %collective-permute-done.9.refs_4_), channel_id=1, source_target_pairs={{0,8},{8,0},{16,24},{24,16},{1,9},{9,1},{17,25},{25,17},{2,10},{10... | collective-permute-start | bytes 786440 | tf_op jit(solution)/shard_map/ppermute | solution.py:158
  27.9 2.2 %collective-permute-start.12 = (f32[128,512]{1,0:T(8,128)S(1)}, f32[128,512]{1,0:T(8,128)S(1)}, u32[]{:S(2)}, u32[]{:S(2)}) collective-permute-start(f32[128,512]{1,0:T(8,128)S(1)} %get-tuple-element.43.refs_2_), channel_id=1, source_target_pairs={{0,8},{8,0},{16,24},{24,16},{1,9},{9,1},{17,25},{25,17},{2,10},{10... | collective-permute-start | bytes 786440 | tf_op jit(solution)/shard_map/ppermute | solution.py:158
  27.9 2.2 %collective-permute-start.14 = (f32[128,512]{1,0:T(8,128)S(1)}, f32[128,512]{1,0:T(8,128)S(1)}, u32[]{:S(2)}, u32[]{:S(2)}) collective-permute-start(f32[128,512]{1,0:T(8,128)S(1)} %collective-permute-done.13.refs_4_), channel_id=1, source_target_pairs={{0,8},{8,0},{16,24},{24,16},{1,9},{9,1},{17,25},{25,17},{2,10},{10... | collective-permute-start | bytes 786440 | tf_op jit(solution)/shard_map/ppermute | solution.py:158
  30.8 11.1 %collective-permute-start.15 = (f32[128,512]{1,0:T(8,128)S(1)}, f32[128,512]{1,0:T(8,128)S(1)}, u32[]{:S(2)}, u32[]{:S(2)}) collective-permute-start(f32[128,512]{1,0:T(8,128)S(1)} %get-tuple-element.28), channel_id=1, source_target_pairs={{0,1},{3,4},{6,7},{8,9},{11,12},{14,15},{16,17},{19,20},{22,23},{2... | collective-permute-start | bytes 786440 | tf_op jit(solution)/shard_map/ppermute | solution.py:155
  32.1 14.4 %collective-permute-start.11 = (f32[128,512]{1,0:T(8,128)S(1)}, f32[128,512]{1,0:T(8,128)S(1)}, u32[]{:S(2)}, u32[]{:S(2)}) collective-permute-start(f32[128,512]{1,0:T(8,128)S(1)} %get-tuple-element.26), channel_id=1, source_target_pairs={{0,1},{3,4},{6,7},{8,9},{11,12},{14,15},{16,17},{19,20},{22,23},{2... | collective-permute-start | bytes 786440 | tf_op jit(solution)/shard_map/ppermute | solution.py:155
  33.4 13.1 %collective-permute-start.16 = (f32[128,512]{1,0:T(8,128)S(1)}, f32[128,512]{1,0:T(8,128)S(1)}, u32[]{:S(2)}, u32[]{:S(2)}) collective-permute-start(f32[128,512]{1,0:T(8,128)S(1)} %get-tuple-element.24.own0), channel_id=1, source_target_pairs={{3,1},{6,4},{11,9},{14,12},{19,17},{22,20},{27,25},{30,28}} | collective-permute-start | bytes 786440 | tf_op jit(solution)/shard_map/ppermute | solution.py:155
  47.6 2.7 %collective-permute-start.17 = (f32[128,512]{1,0:T(8,128)S(1)}, f32[128,512]{1,0:T(8,128)S(1)}, u32[]{:S(2)}, u32[]{:S(2)}) collective-permute-start(f32[128,512]{1,0:T(8,128)S(1)} %get-tuple-element.38), channel_id=1, source_target_pairs={{1,2},{4,5},{9,10},{12,13},{17,18},{20,21},{25,26},{28,29}} | collective-permute-start | bytes 786440 | tf_op jit(solution)/shard_map/ppermute | solution.py:155
  48.3 2.0 %collective-permute-start.18 = (f32[128,512]{1,0:T(8,128)S(1)}, f32[128,512]{1,0:T(8,128)S(1)}, u32[]{:S(2)}, u32[]{:S(2)}) collective-permute-start(f32[128,512]{1,0:T(8,128)S(1)} %get-tuple-element.39), channel_id=1, source_target_pairs={{1,2},{4,5},{9,10},{12,13},{17,18},{20,21},{25,26},{28,29}} | collective-permute-start | bytes 786440 | tf_op jit(solution)/shard_map/ppermute | solution.py:155
  49.0 6.5 %collective-permute-start.19 = (f32[128,512]{1,0:T(8,128)S(1)}, f32[128,512]{1,0:T(8,128)S(1)}, u32[]{:S(2)}, u32[]{:S(2)}) collective-permute-start(f32[128,512]{1,0:T(8,128)S(1)} %get-tuple-element.37.own1), channel_id=1, source_target_pairs={{4,2},{7,5},{12,10},{15,13},{20,18},{23,21},{28,26},{31,29}} | collective-permute-start | bytes 786440 | tf_op jit(solution)/shard_map/ppermute | solution.py:155
  56.0 2.0 %collective-permute-start.20 = (f32[128,512]{1,0:T(8,128)S(1)}, f32[128,512]{1,0:T(8,128)S(1)}, u32[]{:S(2)}, u32[]{:S(2)}) collective-permute-start(f32[128,512]{1,0:T(8,128)S(1)} %get-tuple-element.41), channel_id=1, source_target_pairs={{2,3},{5,6},{10,11},{13,14},{18,19},{21,22},{26,27},{29,30}} | collective-permute-start | bytes 786440 | tf_op jit(solution)/shard_map/ppermute | solution.py:155
  56.7 20.5 %collective-permute-start.21 = (f32[128,512]{1,0:T(8,128)S(1)}, f32[128,512]{1,0:T(8,128)S(1)}, u32[]{:S(2)}, u32[]{:S(2)}) collective-permute-start(f32[128,512]{1,0:T(8,128)S(1)} %get-tuple-element.42), channel_id=1, source_target_pairs={{2,4},{5,7},{10,12},{13,15},{18,20},{21,23},{26,28},{29,31}} | collective-permute-start | bytes 786440 | tf_op jit(solution)/shard_map/ppermute | solution.py:155

commit v2 on v1

v2 whole, which is shorter than its diff:
```python
import functools

import jax
import jax.numpy as jnp
from jax import lax
from jax.experimental import pallas as pl
from jax.experimental.pallas import tpu as pltpu
from jax.sharding import PartitionSpec as P


FACTORS = 4
TICKS = 3


def split_halves(value):
    high = value.astype(jnp.bfloat16)
    low = (value - high.astype(jnp.float32)).astype(jnp.bfloat16)
    return high, low


def product(former, high_ref, low_ref):
    rows = former.shape[0]
    high, low = split_halves(former)
    both = jnp.concatenate([high, low], 0)
    first = jnp.dot(both, high_ref[...], preferred_element_type=jnp.float32)
    second = jnp.dot(high, low_ref[...], preferred_element_type=jnp.float32)
    return first[:rows] + (first[rows:] + second)


def place(groups, offsets_ref):
    column = lax.axis_index("col")
    offset = offsets_ref[column]
    last = 2 * groups - 2 - 2 * column - offset
    return column, lax.rem(column, TICKS), offset, last


def convert(pieces, index, high_ref, low_ref):
    height = pieces[0].shape[1]
    row = lax.axis_index("row")
    for mask, piece in enumerate(pieces):
        high, low = split_halves(piece[index[mask]])
        start = pl.multiple_of((row ^ mask) * height, height)
        high_ref[pl.ds(start, height), :] = high
        low_ref[pl.ds(start, height), :] = low


def strips(first, count, stride):
    return (slice(None), pl.ds(pl.multiple_of(first * stride, stride), count * stride))


def early_kernel(groups, ring, numbers, stride, *refs):
    half = ring // 2
    refs = list(refs)
    offsets_ref = refs.pop(0)
    shift = numbers[0]
    blocks = [refs.pop(0) for _ in range(3 if shift == 0 else 1)]
    pieces = [refs.pop(0) for _ in range(ring)]
    bundled = [refs.pop(0)] if shift == 3 else []
    results = [refs.pop(0) for _ in range(2)]
    *kept, buf = refs
    _, tick, offset, last = place(groups, offsets_ref)
    active = tick == 0

    @pl.when(active)
    def _():
        width = blocks[0].shape[1]
        for i, block in enumerate(blocks):
            buf[:, i * width : (i + 1) * width] = block[...]

    for i, number in enumerate(numbers):
        index = [number] * half + [i] * half
        if shift == 0:
            convert(pieces, index, kept[2 * i], kept[2 * i + 1])

        @pl.when(active & (number <= last))
        def _():
            if shift != 0:
                convert(pieces, index, kept[2 * i], kept[2 * i + 1])
            begin = 0 if shift == 3 else offset + number - shift
            here = strips(begin, 2, stride)
            buf[here] = product(buf[here], kept[2 * i], kept[2 * i + 1])

    @pl.when(active)
    def _():
        if shift == 0:
            results[0][...] = buf[:, : 2 * stride]
            results[1][...] = buf[:, 2 * stride :]
        elif shift == 2:
            results[0][:, :stride] = buf[:, :stride]
            results[0][:, stride:] = buf[strips(3 - 2 * offset, 1, stride)]
            results[1][...] = buf[strips(1 + offset, 2, stride)]
        else:
            results[0][...] = buf[...]

    if bundled:

        @pl.when(tick == 1)
        def _():
            results[1][:1] = bundled[0][...]
            results[1][1:] = pieces[half][...]


def ready_kernel(ring, *refs):
    tick = lax.rem(lax.axis_index("col"), TICKS)
    half = ring // 2
    sets = [refs[i * ring : (i + 1) * ring] for i in range(3)]
    kept = refs[3 * ring :]

    @pl.when(tick == TICKS - 1)
    def _():
        convert(sets[0], [0] * ring, *kept[:2])
        convert(sets[0], [1] * ring, *kept[2:4])
        convert(sets[1], [2] * half + [0] * half, *kept[4:6])
        convert(sets[2], [3] * half + [0] * half, *kept[6:8])


def middle_kernel(groups, stride, *refs):
    offsets_ref, outer, final = refs[:3]
    weights = refs[3 : 3 + FACTORS]
    own, onward, buf = refs[3 + FACTORS :]
    column, tick, offset, last = place(groups, offsets_ref)
    before = offsets_ref[jnp.maximum(column - 1, 0)]

    @pl.when(tick == 1)
    def _():
        buf[:, :stride] = outer[:, :stride]
        buf[strips(3 - 2 * before, 1, stride)] = outer[:, stride:]
        buf[strips(1 + before, 2, stride)] = final[...]
        for number in range(FACTORS // 2):

            @pl.when(number <= last)
            def _():
                here = strips(offset + number, 2, stride)
                buf[here] = product(buf[here], weights[2 * number], weights[2 * number + 1])

        own[...] = buf[:, : 2 * stride]
        onward[...] = buf[:, 2 * stride :]


def last_kernel(groups, turns, stride, *refs):
    count, half = len(turns), FACTORS // 2
    offsets_ref, first, second = refs[:3]
    weights = refs[3 : 3 + 2 * count]
    *results, buf = refs[3 + 2 * count :]
    column, tick, offset, last = place(groups, offsets_ref)
    before = offsets_ref[jnp.maximum(column - 1, 0)]

    @pl.when(tick == TICKS - 1)
    def _():
        buf[:, : 2 * stride] = first[...]
        buf[:, 2 * stride :] = second[...]
        for i, turn in enumerate(turns):
            if turn < half:
                start = before + turn
                valid = turn + half <= last + 2 + offset - before
            else:
                start = offset + turn - half - (half if turns[0] else 0)
                valid = turn - half <= last

            @pl.when(valid)
            def _():
                here = strips(start, 2, stride)
                buf[here] = product(buf[here], weights[2 * i], weights[2 * i + 1])

        results[0][...] = buf[:, : 2 * stride]
        results[1][...] = buf[:, 2 * stride :]


def pick_kernel(own0, own1, own2, near, far, out):
    column = lax.axis_index("col")
    tick = lax.rem(column, TICKS)
    for source, chosen in (
        (own0, (tick == 0) & (column < TICKS)),
        (near, (tick == 0) & (column >= TICKS)),
        (own1, (tick == 1) & (column < TICKS)),
        (far, (tick == 1) & (column >= TICKS)),
        (own2, tick == 2),
    ):

        @pl.when(chosen)
        def _():
            out[...] = source[...]


def on_device(groups, ring, vectors, factors, offsets):
    rows, width = vectors.shape
    stride = width // 2
    height = factors.shape[2]
    order = ring * height
    f32, bf16 = jnp.float32, jnp.bfloat16
    on_chip = pl.BlockSpec(memory_space=pltpu.VMEM)
    scalars = pl.BlockSpec(memory_space=pltpu.SMEM)
    bits = [1 << i for i in range(ring.bit_length() - 1)]
    top = bits.pop()

    def along(array, distance, tick):
        pairs = [
            (i, i + distance)
            for i in range(groups)
            if i % TICKS == tick and 0 <= i + distance < groups
        ]
        return lax.ppermute(array, "col", pairs)

    def across(array, moves):
        pairs = [
            (row * groups + source, (row ^ top) * groups + target)
            for row in range(ring)
            for source, target in moves
        ]
        return lax.ppermute(array, ("row", "col"), pairs)

    def spread(pieces):
        for bit in bits[::-1]:
            for mask in list(pieces):
                pieces[mask ^ bit] = lax.ppermute(
                    pieces[mask], "row", [(i, i ^ bit) for i in range(ring)]
                )
        return [pieces[mask] for mask in sorted(pieces)]

    def call(kernel, outs, scratch, *operands):
        return pl.pallas_call(
            kernel,
            out_shape=outs,
            in_specs=[scalars if op.dtype == jnp.int32 else on_chip for op in operands],
            out_specs=[on_chip] * len(outs),
            scratch_shapes=scratch,
            compiler_params=pltpu.CompilerParams(vmem_limit_bytes=24 << 20),
        )(*operands)

    def block(columns=width, dtype=f32, high=rows):
        return jax.ShapeDtypeStruct((high, columns), dtype)

    def pair(count):
        return [block(order, bf16, order)] * (2 * count)

    half = FACTORS // 2
    whole = factors[0]
    same = [(i, i) for i in range(groups)]
    own = spread({0: whole})
    cuts = {0: whole[:half], 2: whole[2:3], 3: whole[3:]}
    away = {number: across(cut, same) for number, cut in cuts.items()}
    gathered = {number: own + spread({top: cut}) for number, cut in away.items()}
    handed = spread({0: along(whole[half:], 1, 1)})

    beside = along(vectors, -1, 1)
    distant = along(vectors, -2, 2)

    def early(numbers, blocks, outs, *more):
        span = sum(b.shape[1] for b in blocks)
        return call(
            functools.partial(early_kernel, groups, ring, numbers, stride),
            outs,
            ([] if blocks[1:] else [pltpu.VMEM((order, order), bf16)] * 2)
            + [pltpu.VMEM((rows, span), f32)],
            offsets,
            *blocks,
            *gathered[numbers[0]],
            *more,
        )

    own0, rest, *first_pairs = early(
        (0, 1), [vectors, beside, distant], [block(), block(2 * width), *pair(2)]
    )
    third = along(own0, -1, 0)
    outer, passing = early((2,), [rest], [block(), block()])
    outer = along(outer, 1, 0)
    bundle = jax.ShapeDtypeStruct((half, height, order), f32)
    final, bundle = early((3,), [passing], [block(), bundle], away[2])
    final = along(final, 1, 0)
    handed += spread({top: along(bundle, 1, 1)})

    second_pairs = call(
        functools.partial(ready_kernel, ring),
        pair(FACTORS),
        [],
        *handed,
        *gathered[2],
        *gathered[3],
    )
    own1, onward = call(
        functools.partial(middle_kernel, groups, stride),
        [block()] * 2,
        [pltpu.VMEM((rows, 2 * width), f32)],
        offsets,
        outer,
        final,
        *first_pairs,
    )
    onward = along(onward, 1, 1)
    fourth = along(own1, -2, 1)
    own2, near = call(
        functools.partial(last_kernel, groups, (0, 1, 2, 3), stride),
        [block()] * 2,
        [pltpu.VMEM((rows, 2 * width), f32)],
        offsets,
        onward,
        third,
        *second_pairs[: 2 * half],
        *first_pairs,
    )
    near, far = call(
        functools.partial(last_kernel, groups, (4, 5), stride),
        [block()] * 2,
        [pltpu.VMEM((rows, 2 * width), f32)],
        offsets,
        near,
        fourth,
        *second_pairs[2 * half :],
    )
    near = along(near, 1, 2)
    far = along(far, 2, 2)
    (out,) = call(pick_kernel, [block()], [], own0, own1, own2, near, far)
    return out


def solution(mesh):
    placed = (P("row", "col"), P("col", None, "row", None), P())
    ring = mesh.shape["row"]

    def body(*blocks):
        return on_device(mesh.shape["col"], ring, *blocks)

    return jax.shard_map(
        body, mesh=mesh, in_specs=placed, out_specs=P("row", "col"), check_vma=False
    )
```

time: 78.2 us -> 92.4 us (1.18)
  starting transfers between devices: 16.7 us -> 26.2 us
  waiting for transfers between devices: 55.1 us -> 59.4 us
    ppermute x10 -> x11, starting transfers between devices: 11 us -> 21.9 us  [along(): return lax.ppermute(array, 'col', pairs)]
    ppermute x12 -> x9, waiting for transfers between devices: 18.2 us -> 21.3 us  [the longest x3 21.3 us: across(): return lax.ppermute(array, ('row', 'col'), pairs)]
    ppermute x12 -> x9, starting transfers between devices: 5.72 us -> 4.25 us  [the longest x3 3.58 us: across(): return lax.ppermute(array, ('row', 'col'), pairs)]
    slice x0 -> x2, local copies, waits for them, and re-layouts: none -> 1.41 us  [the longest x1 1.38 us: on_device(): handed = spread({0: along(whole[half:], 1, 1)})]
    squeeze x1 -> x0, local copies, waits for them, and re-layouts: 1.3 us -> none  [on_device(): pieces = {0: factors[0, number]}]
    ppermute x10 -> x11, waiting for transfers between devices: 36.8 us -> 38.1 us  [along(): return lax.ppermute(array, 'col', pairs)]
    pallas_call x6 -> x8, Pallas kernels: 4.69 us -> 4.94 us  [call(): pl.pallas_call(kernel, out_shape=outs, in_specs=[scalars if op.dtype == j...]
  transfers between devices with their start and end apart: 22 -> 20, of which waited for: 8 -> 7; matrix products, arithmetic and copies ran while one was open for 0% -> 0% of each run, Pallas kernels for 2% -> 4%
where the time goes in v2:
time: 92.4 us; the launch traced here: 92.2 us
  waiting for transfers between devices  59.4 us (64%)
  starting transfers between devices  26.2 us (28%)
  Pallas kernels  4.94 us (5%)
  local copies, waits for them, and re-layouts  1.43 us (2%)
    ppermute x11, waiting for transfers between devices, along(): return lax.ppermute(array, 'col', pairs)  38.1 us
    ppermute x11, starting transfers between devices, along(): return lax.ppermute(array, 'col', pairs)  21.9 us
    ppermute x3, waiting for transfers between devices, across(): return lax.ppermute(array, ('row', 'col'), pairs)  21.3 us
    pallas_call x8, Pallas kernels, call(): pl.pallas_call(kernel, out_shape=outs, in_specs=[scalars if op.dtype == j...  4.94 us
    ppermute x3, starting transfers between devices, across(): return lax.ppermute(array, ('row', 'col'), pairs)  3.58 us
  transfers between devices with their start and end apart: 20, of which 7 were waited for; matrix products, arithmetic and copies ran while one was open for 0% of the time, Pallas kernels for 4%

profile of v2, /device:TPU:28, one launch (start us, length us, event | category | flops | bytes accessed | tf_op | source)
XLA Modules:
  0.0 92.2 jit_solution(1388654734722067802)
XLA Ops:
  0.0 1.4 %slice_bitcast_fusion = (f32[2,128,512]{2,1,0:T(8,128)S(1)}, f32[2,128,512]{2,1,0:T(8,128)S(1)}) fusion(f32[1,4,128,512]{3,2,1,0:T(8,128)} %param.4), kind=kLoop, calls=%fused_computation | loop fusion | bytes 2097152 | tf_op jit(solution)/shard_map/slice | solution.py:243
  1.4 1.6 %collective-permute-start.3 = (f32[2,128,512]{2,1,0:T(8,128)S(1)}, f32[2,128,512]{2,1,0:T(8,128)S(1)}, u32[]{:S(2)}, u32[]{:S(2)}) collective-permute-start(f32[2,128,512]{2,1,0:T(8,128)S(1)} %get-tuple-element.54), channel_id=1, source_target_pairs={{0,16},{1,17},{2,18},{3,19},{4,20},{5,21},{6,22},{7,23},{8,24},{9,... | collective-permute-start | bytes 1572872 | tf_op jit(solution)/shard_map/ppermute | solution.py:210
  3.0 2.4 %collective-permute-start = (f32[128,512]{1,0:T(8,128)S(1)}, f32[128,512]{1,0:T(8,128)S(1)}, u32[]{:S(2)}, u32[]{:S(2)}) collective-permute-start(f32[128,512]{1,0:T(8,128)S(1)} %copy-done.1), channel_id=1, source_target_pairs={{1,0},{4,3},{7,6},{9,8},{12,11},{15,14},{17,16},{20,19},{23,22},{2... | collective-permute-start | bytes 786440 | tf_op jit(solution)/shard_map/ppermute | solution.py:202
  5.4 9.7 %collective-permute-done.3.refs_6_ = f32[2,128,512]{2,1,0:T(8,128)S(1)} collective-permute-done((f32[2,128,512]{2,1,0:T(8,128)S(1)}, f32[2,128,512]{2,1,0:T(8,128)S(1)}, u32[]{:S(2)}, u32[]{:S(2)}) %collective-permute-start.3) | collective-permute-done | bytes 524320 | tf_op jit(solution)/shard_map/ppermute | solution.py:210
  15.1 1.5 %collective-permute-start.5 = (f32[1,128,512]{2,1,0:T(8,128)S(1)}, f32[1,128,512]{2,1,0:T(8,128)S(1)}, u32[]{:S(2)}, u32[]{:S(2)}) collective-permute-start(f32[1,128,512]{2,1,0:T(8,128)S(1)} %get-tuple-element.56), channel_id=1, source_target_pairs={{0,16},{1,17},{2,18},{3,19},{4,20},{5,21},{6,22},{7,23},{8,24},{9,... | collective-permute-start | bytes 786440 | tf_op jit(solution)/shard_map/ppermute | solution.py:210
  17.2 0.7 collective-permute-start.1
  17.8 6.5 %collective-permute-done.5.refs_4_.refs_6_ = f32[1,128,512]{2,1,0:T(8,128)S(1)} collective-permute-done((f32[1,128,512]{2,1,0:T(8,128)S(1)}, f32[1,128,512]{2,1,0:T(8,128)S(1)}, u32[]{:S(2)}, u32[]{:S(2)}) %collective-permute-start.5) | collective-permute-done | bytes 262176 | tf_op jit(solution)/shard_map/ppermute | solution.py:210
  24.3 5.2 %collective-permute-done.8.refs_4_.refs_10_ = f32[1,128,512]{2,1,0:T(8,128)S(1)} collective-permute-done((f32[1,128,512]{2,1,0:T(8,128)S(1)}, f32[1,128,512]{2,1,0:T(8,128)S(1)}, u32[]{:S(2)}, u32[]{:S(2)}) %collective-permute-start.8) | collective-permute-done | bytes 262176 | tf_op jit(solution)/shard_map/ppermute | solution.py:210
  29.5 0.7 collective-permute-start.13
  30.2 0.9 shard_map.37
  32.3 0.7 collective-permute-start.15
  33.0 1.3 %collective-permute-start.10 = (f32[128,512]{1,0:T(8,128)S(1)}, f32[128,512]{1,0:T(8,128)S(1)}, u32[]{:S(2)}, u32[]{:S(2)}) collective-permute-start(f32[128,512]{1,0:T(8,128)S(1)} %get-tuple-element.33), channel_id=1, source_target_pairs={{0,1},{3,4},{6,7},{8,9},{11,12},{14,15},{16,17},{19,20},{22,23},{2... | collective-permute-start | bytes 786440 | tf_op jit(solution)/shard_map/ppermute | solution.py:202
  34.3 1.3 %collective-permute-start.7 = (f32[128,512]{1,0:T(8,128)S(1)}, f32[128,512]{1,0:T(8,128)S(1)}, u32[]{:S(2)}, u32[]{:S(2)}) collective-permute-start(f32[128,512]{1,0:T(8,128)S(1)} %get-tuple-element.31), channel_id=1, source_target_pairs={{0,1},{3,4},{6,7},{8,9},{11,12},{14,15},{16,17},{19,20},{22,23},{2... | collective-permute-start | bytes 786440 | tf_op jit(solution)/shard_map/ppermute | solution.py:202
  36.3 0.7 collective-permute-start.12
  37.0 7.1 %collective-permute-done.10.refs_2_ = f32[128,512]{1,0:T(8,128)S(1)} collective-permute-done((f32[128,512]{1,0:T(8,128)S(1)}, f32[128,512]{1,0:T(8,128)S(1)}, u32[]{:S(2)}, u32[]{:S(2)}) %collective-permute-start.10) | collective-permute-done | bytes 262176 | tf_op jit(solution)/shard_map/ppermute | solution.py:202
  44.1 5.2 %collective-permute-done.7.refs_1_ = f32[128,512]{1,0:T(8,128)S(1)} collective-permute-done((f32[128,512]{1,0:T(8,128)S(1)}, f32[128,512]{1,0:T(8,128)S(1)}, u32[]{:S(2)}, u32[]{:S(2)}) %collective-permute-start.7) | collective-permute-done | bytes 262176 | tf_op jit(solution)/shard_map/ppermute | solution.py:202
  49.2 1.0 %shard_map.40 = (f32[128,512]{1,0:T(8,128)S(1)}, f32[128,512]{1,0:T(8,128)S(1)}) custom-call(s32[8]{0:T(128)S(1)} %copy-done.2, f32[128,512]{1,0:T(8,128)S(1)} %collective-permute-done.7.refs_1_, f32[128,512]{1,0:T(8,128)S(1)} %collective-permute-done.10.refs_2_, bf16[512,512]{1,0:T(8,128)(2,1)S(1)} %get-tuple-element.34.refs_3_.refs_7_, ...), custom_call_target="tpu_custom_call" | custom-call | tf_op jit(solution)/shard_map/pallas_call | solution.py:221
  50.2 0.7 collective-permute-start.11
  50.9 11.6 %collective-permute-start.17 = (f32[128,512]{1,0:T(8,128)S(1)}, f32[128,512]{1,0:T(8,128)S(1)}, u32[]{:S(2)}, u32[]{:S(2)}) collective-permute-start(f32[128,512]{1,0:T(8,128)S(1)} %get-tuple-element.38.own1), channel_id=1, source_target_pairs={{4,2},{7,5},{12,10},{15,13},{20,18},{23,21},{28,26},{31,29}} | collective-permute-start | bytes 786440 | tf_op jit(solution)/shard_map/ppermute | solution.py:202
  63.1 5.6 %collective-permute-done.17.refs_2_ = f32[128,512]{1,0:T(8,128)S(1)} collective-permute-done((f32[128,512]{1,0:T(8,128)S(1)}, f32[128,512]{1,0:T(8,128)S(1)}, u32[]{:S(2)}, u32[]{:S(2)}) %collective-permute-start.17) | collective-permute-done | bytes 262176 | tf_op jit(solution)/shard_map/ppermute | solution.py:202
  69.3 0.7 collective-permute-start.18
  69.9 1.3 %collective-permute-start.19 = (f32[128,512]{1,0:T(8,128)S(1)}, f32[128,512]{1,0:T(8,128)S(1)}, u32[]{:S(2)}, u32[]{:S(2)}) collective-permute-start(f32[128,512]{1,0:T(8,128)S(1)} %get-tuple-element.52), channel_id=1, source_target_pairs={{2,4},{5,7},{10,12},{13,15},{18,20},{21,23},{26,28},{29,31}} | collective-permute-start | bytes 786440 | tf_op jit(solution)/shard_map/ppermute | solution.py:202
  71.2 20.2 %collective-permute-done.19.far = f32[128,512]{1,0:T(8,128)S(1)} collective-permute-done((f32[128,512]{1,0:T(8,128)S(1)}, f32[128,512]{1,0:T(8,128)S(1)}, u32[]{:S(2)}, u32[]{:S(2)}) %collective-permute-start.19) | collective-permute-done | bytes 262176 | tf_op jit(solution)/shard_map/ppermute | solution.py:202
  91.4 0.7 shard_map.44
  (32 shorter events, 3.6 us)
Async XLA Ops:
  0.0 2.9 %copy-start = (f32[1,4,128,512]{3,2,1,0:T(8,128)S(1)}, f32[1,4,128,512]{3,2,1,0:T(8,128)}, u32[]{:S(2)}) copy-start(f32[1,4,128,512]{3,2,1,0:T(8,128)} %param.4) | copy-start | bytes 3145732
  0.0 3.0 %copy-start.1 = (f32[128,512]{1,0:T(8,128)S(1)}, f32[128,512]{1,0:T(8,128)}, u32[]{:S(2)}) copy-start(f32[128,512]{1,0:T(8,128)} %refs_1_.1) | copy-start | bytes 786436
  1.4 13.7 %collective-permute-start.3 = (f32[2,128,512]{2,1,0:T(8,128)S(1)}, f32[2,128,512]{2,1,0:T(8,128)S(1)}, u32[]{:S(2)}, u32[]{:S(2)}) collective-permute-start(f32[2,128,512]{2,1,0:T(8,128)S(1)} %get-tuple-element.54), channel_id=1, source_target_pairs={{0,16},{1,17},{2,18},{3,19},{4,20},{5,21},{6,22},{7,23},{8,24},{9,... | collective-permute-start | bytes 1572872 | tf_op jit(solution)/shard_map/ppermute | solution.py:210
  3.0 27.2 %collective-permute-start.2 = (f32[4,128,512]{2,1,0:T(8,128)S(1)}, f32[4,128,512]{2,1,0:T(8,128)S(1)}, u32[]{:S(2)}, u32[]{:S(2)}) collective-permute-start(f32[4,128,512]{2,1,0:T(8,128)S(1)} %bitcast.9), channel_id=1, source_target_pairs={{0,8},{8,0},{16,24},{24,16},{1,9},{9,1},{17,25},{25,17},{2,10},{10... | collective-permute-start | bytes 3145736 | tf_op jit(solution)/shard_map/ppermute | solution.py:215
  3.0 14.2 %collective-permute-start = (f32[128,512]{1,0:T(8,128)S(1)}, f32[128,512]{1,0:T(8,128)S(1)}, u32[]{:S(2)}, u32[]{:S(2)}) collective-permute-start(f32[128,512]{1,0:T(8,128)S(1)} %copy-done.1), channel_id=1, source_target_pairs={{1,0},{4,3},{7,6},{9,8},{12,11},{15,14},{17,16},{20,19},{23,22},{2... | collective-permute-start | bytes 786440 | tf_op jit(solution)/shard_map/ppermute | solution.py:202
  15.1 15.1 %collective-permute-start.4 = (f32[2,128,512]{2,1,0:T(8,128)S(1)}, f32[2,128,512]{2,1,0:T(8,128)S(1)}, u32[]{:S(2)}, u32[]{:S(2)}) collective-permute-start(f32[2,128,512]{2,1,0:T(8,128)S(1)} %collective-permute-done.3.refs_6_), channel_id=1, source_target_pairs={{0,8},{8,0},{16,24},{24,16},{1,9},{9,1},{17,25},{25,17},{2,10},{10... | collective-permute-start | bytes 1572872 | tf_op jit(solution)/shard_map/ppermute | solution.py:215
  15.1 9.2 %collective-permute-start.5 = (f32[1,128,512]{2,1,0:T(8,128)S(1)}, f32[1,128,512]{2,1,0:T(8,128)S(1)}, u32[]{:S(2)}, u32[]{:S(2)}) collective-permute-start(f32[1,128,512]{2,1,0:T(8,128)S(1)} %get-tuple-element.56), channel_id=1, source_target_pairs={{0,16},{1,17},{2,18},{3,19},{4,20},{5,21},{6,22},{7,23},{8,24},{9,... | collective-permute-start | bytes 786440 | tf_op jit(solution)/shard_map/ppermute | solution.py:210
  16.6 13.6 %copy-start.2 = (s32[8]{0:T(128)S(1)}, s32[8]{0:T(128)}, u32[]{:S(2)}) copy-start(s32[8]{0:T(128)} %refs_0_.11) | copy-start | bytes 100
  16.6 12.8 %collective-permute-start.8 = (f32[1,128,512]{2,1,0:T(8,128)S(1)}, f32[1,128,512]{2,1,0:T(8,128)S(1)}, u32[]{:S(2)}, u32[]{:S(2)}) collective-permute-start(f32[1,128,512]{2,1,0:T(8,128)S(1)} %get-tuple-element.55), channel_id=1, source_target_pairs={{0,16},{1,17},{2,18},{3,19},{4,20},{5,21},{6,22},{7,23},{8,24},{9,... | collective-permute-start | bytes 786440 | tf_op jit(solution)/shard_map/ppermute | solution.py:210
  17.2 12.3 %collective-permute-start.1 = (f32[128,512]{1,0:T(8,128)S(1)}, f32[128,512]{1,0:T(8,128)S(1)}, u32[]{:S(2)}, u32[]{:S(2)}) collective-permute-start(f32[128,512]{1,0:T(8,128)S(1)} %copy-done.1), channel_id=1, source_target_pairs={{2,0},{5,3},{10,8},{13,11},{18,16},{21,19},{26,24},{29,27}} | collective-permute-start | bytes 786440 | tf_op jit(solution)/shard_map/ppermute | solution.py:202
  24.3 6.8 %collective-permute-start.6 = (f32[1,128,512]{2,1,0:T(8,128)S(1)}, f32[1,128,512]{2,1,0:T(8,128)S(1)}, u32[]{:S(2)}, u32[]{:S(2)}) collective-permute-start(f32[1,128,512]{2,1,0:T(8,128)S(1)} %collective-permute-done.5.refs_4_.refs_6_), channel_id=1, source_target_pairs={{0,8},{8,0},{16,24},{24,16},{1,9},{9,1},{17,25},{25,17},{2,10},{10... | collective-permute-start | bytes 786440 | tf_op jit(solution)/shard_map/ppermute | solution.py:215
  29.5 2.2 %collective-permute-start.9 = (f32[1,128,512]{2,1,0:T(8,128)S(1)}, f32[1,128,512]{2,1,0:T(8,128)S(1)}, u32[]{:S(2)}, u32[]{:S(2)}) collective-permute-start(f32[1,128,512]{2,1,0:T(8,128)S(1)} %collective-permute-done.8.refs_4_.refs_10_), channel_id=1, source_target_pairs={{0,8},{8,0},{16,24},{24,16},{1,9},{9,1},{17,25},{25,17},{2,10},{10... | collective-permute-start | bytes 786440 | tf_op jit(solution)/shard_map/ppermute | solution.py:215
  29.5 6.1 %collective-permute-start.13 = (f32[2,128,512]{2,1,0:T(8,128)S(1)}, f32[2,128,512]{2,1,0:T(8,128)S(1)}, u32[]{:S(2)}, u32[]{:S(2)}) collective-permute-start(f32[2,128,512]{2,1,0:T(8,128)S(1)} %get-tuple-element.53), channel_id=1, source_target_pairs={{1,2},{4,5},{9,10},{12,13},{17,18},{20,21},{25,26},{28,29}} | collective-permute-start | bytes 1572872 | tf_op jit(solution)/shard_map/ppermute | solution.py:202
  32.3 3.9 %collective-permute-start.15 = (f32[2,128,512]{2,1,0:T(8,128)S(1)}, f32[2,128,512]{2,1,0:T(8,128)S(1)}, u32[]{:S(2)}, u32[]{:S(2)}) collective-permute-start(f32[2,128,512]{2,1,0:T(8,128)S(1)} %get-tuple-element.40), channel_id=1, source_target_pairs={{1,2},{4,5},{9,10},{12,13},{17,18},{20,21},{25,26},{28,29}} | collective-permute-start | bytes 1572872 | tf_op jit(solution)/shard_map/ppermute | solution.py:202
  33.0 11.1 %collective-permute-start.10 = (f32[128,512]{1,0:T(8,128)S(1)}, f32[128,512]{1,0:T(8,128)S(1)}, u32[]{:S(2)}, u32[]{:S(2)}) collective-permute-start(f32[128,512]{1,0:T(8,128)S(1)} %get-tuple-element.33), channel_id=1, source_target_pairs={{0,1},{3,4},{6,7},{8,9},{11,12},{14,15},{16,17},{19,20},{22,23},{2... | collective-permute-start | bytes 786440 | tf_op jit(solution)/shard_map/ppermute | solution.py:202
  34.3 14.9 %collective-permute-start.7 = (f32[128,512]{1,0:T(8,128)S(1)}, f32[128,512]{1,0:T(8,128)S(1)}, u32[]{:S(2)}, u32[]{:S(2)}) collective-permute-start(f32[128,512]{1,0:T(8,128)S(1)} %get-tuple-element.31), channel_id=1, source_target_pairs={{0,1},{3,4},{6,7},{8,9},{11,12},{14,15},{16,17},{19,20},{22,23},{2... | collective-permute-start | bytes 786440 | tf_op jit(solution)/shard_map/ppermute | solution.py:202
  35.6 26.9 %collective-permute-start.14 = (f32[2,128,512]{2,1,0:T(8,128)S(1)}, f32[2,128,512]{2,1,0:T(8,128)S(1)}, u32[]{:S(2)}, u32[]{:S(2)}) collective-permute-start(f32[2,128,512]{2,1,0:T(8,128)S(1)} %collective-permute-done.13.refs_0_), channel_id=1, source_target_pairs={{0,8},{8,0},{16,24},{24,16},{1,9},{9,1},{17,25},{25,17},{2,10},{10... | collective-permute-start | bytes 1572872 | tf_op jit(solution)/shard_map/ppermute | solution.py:215
  36.2 26.3 %collective-permute-start.16 = (f32[2,128,512]{2,1,0:T(8,128)S(1)}, f32[2,128,512]{2,1,0:T(8,128)S(1)}, u32[]{:S(2)}, u32[]{:S(2)}) collective-permute-start(f32[2,128,512]{2,1,0:T(8,128)S(1)} %collective-permute-done.15.refs_2_), channel_id=1, source_target_pairs={{0,8},{8,0},{16,24},{24,16},{1,9},{9,1},{17,25},{25,17},{2,10},{10... | collective-permute-start | bytes 1572872 | tf_op jit(solution)/shard_map/ppermute | solution.py:215
  36.3 26.3 %collective-permute-start.12 = (f32[128,512]{1,0:T(8,128)S(1)}, f32[128,512]{1,0:T(8,128)S(1)}, u32[]{:S(2)}, u32[]{:S(2)}) collective-permute-start(f32[128,512]{1,0:T(8,128)S(1)} %get-tuple-element.29.own0), channel_id=1, source_target_pairs={{3,2},{6,5},{11,10},{14,13},{19,18},{22,21},{27,26},{30,29}} | collective-permute-start | bytes 786440 | tf_op jit(solution)/shard_map/ppermute | solution.py:202
  50.2 12.3 %collective-permute-start.11 = (f32[128,512]{1,0:T(8,128)S(1)}, f32[128,512]{1,0:T(8,128)S(1)}, u32[]{:S(2)}, u32[]{:S(2)}) collective-permute-start(f32[128,512]{1,0:T(8,128)S(1)} %get-tuple-element.39), channel_id=1, source_target_pairs={{1,2},{4,5},{9,10},{12,13},{17,18},{20,21},{25,26},{28,29}} | collective-permute-start | bytes 786440 | tf_op jit(solution)/shard_map/ppermute | solution.py:202
  50.9 17.8 %collective-permute-start.17 = (f32[128,512]{1,0:T(8,128)S(1)}, f32[128,512]{1,0:T(8,128)S(1)}, u32[]{:S(2)}, u32[]{:S(2)}) collective-permute-start(f32[128,512]{1,0:T(8,128)S(1)} %get-tuple-element.38.own1), channel_id=1, source_target_pairs={{4,2},{7,5},{12,10},{15,13},{20,18},{23,21},{28,26},{31,29}} | collective-permute-start | bytes 786440 | tf_op jit(solution)/shard_map/ppermute | solution.py:202
  69.3 2.0 %collective-permute-start.18 = (f32[128,512]{1,0:T(8,128)S(1)}, f32[128,512]{1,0:T(8,128)S(1)}, u32[]{:S(2)}, u32[]{:S(2)}) collective-permute-start(f32[128,512]{1,0:T(8,128)S(1)} %get-tuple-element.51), channel_id=1, source_target_pairs={{2,3},{5,6},{10,11},{13,14},{18,19},{21,22},{26,27},{29,30}} | collective-permute-start | bytes 786440 | tf_op jit(solution)/shard_map/ppermute | solution.py:202
  69.9 21.5 %collective-permute-start.19 = (f32[128,512]{1,0:T(8,128)S(1)}, f32[128,512]{1,0:T(8,128)S(1)}, u32[]{:S(2)}, u32[]{:S(2)}) collective-permute-start(f32[128,512]{1,0:T(8,128)S(1)} %get-tuple-element.52), channel_id=1, source_target_pairs={{2,4},{5,7},{10,12},{13,15},{18,20},{21,23},{26,28},{29,31}} | collective-permute-start | bytes 786440 | tf_op jit(solution)/shard_map/ppermute | solution.py:202

commit v3 on v2

--- a/solution.py
+++ b/solution.py
@@ -55,8 +55,7 @@
     shift = numbers[0]
     blocks = [refs.pop(0) for _ in range(3 if shift == 0 else 1)]
     pieces = [refs.pop(0) for _ in range(ring)]
-    bundled = [refs.pop(0)] if shift == 3 else []
-    results = [refs.pop(0) for _ in range(2)]
+    results = [refs.pop(0) for _ in range(1 if shift == 3 else 2)]
     *kept, buf = refs
     _, tick, offset, last = place(groups, offsets_ref)
     active = tick == 0
@@ -92,26 +91,17 @@
         else:
             results[0][...] = buf[...]
 
-    if bundled:
-
-        @pl.when(tick == 1)
-        def _():
-            results[1][:1] = bundled[0][...]
-            results[1][1:] = pieces[half][...]
-
 
 def ready_kernel(ring, *refs):
     tick = lax.rem(lax.axis_index("col"), TICKS)
     half = ring // 2
-    sets = [refs[i * ring : (i + 1) * ring] for i in range(3)]
-    kept = refs[3 * ring :]
+    kept = refs[4 * ring :]
 
     @pl.when(tick == TICKS - 1)
     def _():
-        convert(sets[0], [0] * ring, *kept[:2])
-        convert(sets[0], [1] * ring, *kept[2:4])
-        convert(sets[1], [2] * half + [0] * half, *kept[4:6])
-        convert(sets[2], [3] * half + [0] * half, *kept[6:8])
+        for i, own in enumerate((0, 1, 2, 3)):
+            pieces = refs[i * ring : (i + 1) * ring]
+            convert(pieces, [own] * half + [0] * half, *kept[2 * i : 2 * i + 2])
 
 
 def middle_kernel(groups, stride, *refs):
@@ -193,13 +183,27 @@
     bits = [1 << i for i in range(ring.bit_length() - 1)]
     top = bits.pop()
 
-    def along(array, distance, tick):
-        pairs = [
-            (i, i + distance)
+    def along(array, distance, tick, back="straight"):
+        swaps = {
+            i: i + distance
             for i in range(groups)
             if i % TICKS == tick and 0 <= i + distance < groups
+        }
+        moves = {i: i for i in range(groups)}
+        for source, target in swaps.items():
+            if back == "none":
+                moves |= {source: target}
+                del moves[target]
+            elif back == "straight":
+                moves |= {source: target, target: source}
+            else:
+                moves |= {source: target, target: source - 1, source - 1: source}
+        pairs = [
+            (row * groups + i, (row ^ 1 if i == target else row) * groups + target)
+            for row in range(ring)
+            for i, target in moves.items()
         ]
-        return lax.ppermute(array, "col", pairs)
+        return lax.ppermute(array, ("row", "col"), pairs)
 
     def across(array, moves):
         pairs = [
@@ -240,12 +244,12 @@
     cuts = {0: whole[:half], 2: whole[2:3], 3: whole[3:]}
     away = {number: across(cut, same) for number, cut in cuts.items()}
     gathered = {number: own + spread({top: cut}) for number, cut in away.items()}
-    handed = spread({0: along(whole[half:], 1, 1)})
+    handed = spread({0: along(whole[half:], 1, 1, "none")})
 
     beside = along(vectors, -1, 1)
     distant = along(vectors, -2, 2)
 
-    def early(numbers, blocks, outs, *more):
+    def early(numbers, blocks, outs):
         span = sum(b.shape[1] for b in blocks)
         return call(
             functools.partial(early_kernel, groups, ring, numbers, stride),
@@ -255,7 +259,6 @@
             offsets,
             *blocks,
             *gathered[numbers[0]],
-            *more,
         )
 
     own0, rest, *first_pairs = early(
@@ -264,16 +267,21 @@
     third = along(own0, -1, 0)
     outer, passing = early((2,), [rest], [block(), block()])
     outer = along(outer, 1, 0)
-    bundle = jax.ShapeDtypeStruct((half, height, order), f32)
-    final, bundle = early((3,), [passing], [block(), bundle], away[2])
+    (final,) = early((3,), [passing], [block()])
     final = along(final, 1, 0)
-    handed += spread({top: along(bundle, 1, 1)})
+    passed = {
+        number: spread({top: along(away[number], 1, 1, "none")})
+        for number in range(half, FACTORS)
+    }
 
     second_pairs = call(
         functools.partial(ready_kernel, ring),
         pair(FACTORS),
         [],
         *handed,
+        *passed[2],
+        *handed,
+        *passed[3],
         *gathered[2],
         *gathered[3],
     )
@@ -286,8 +294,8 @@
         final,
         *first_pairs,
     )
-    onward = along(onward, 1, 1)
-    fourth = along(own1, -2, 1)
+    onward = along(onward, 1, 1, "leader")
+    fourth = along(own1, -2, 1, "none")
     own2, near = call(
         functools.partial(last_kernel, groups, (0, 1, 2, 3), stride),
         [block()] * 2,

time: 92.4 us -> 80.7 us (0.87)
  starting transfers between devices: 26.2 us -> 18.1 us
  waiting for transfers between devices: 59.4 us -> 55.8 us
    ppermute x11 -> x12, starting transfers between devices: 21.9 us -> 13.9 us  [along(): return lax.ppermute(array, ('row', 'col'), pairs)]
    ppermute x11 -> x12, waiting for transfers between devices: 38.1 us -> 34 us  [along(): return lax.ppermute(array, ('row', 'col'), pairs)]
  transfers between devices with their start and end apart: 20 -> 22, of which waited for: 7 -> 8; matrix products, arithmetic and copies ran while one was open for 0% -> 0% of each run, Pallas kernels for 4% -> 4%
where the time goes in v3:
time: 80.7 us; the launch traced here: 80.5 us
  waiting for transfers between devices  55.8 us (69%)
  starting transfers between devices  18.1 us (22%)
  Pallas kernels  4.9 us (6%)
  local copies, waits for them, and re-layouts  1.43 us (2%)
    ppermute x12, waiting for transfers between devices, along(): return lax.ppermute(array, ('row', 'col'), pairs)  34 us
    ppermute x3, waiting for transfers between devices, across(): return lax.ppermute(array, ('row', 'col'), pairs)  21.8 us
    ppermute x12, starting transfers between devices, along(): return lax.ppermute(array, ('row', 'col'), pairs)  13.9 us
    pallas_call x8, Pallas kernels, call(): pl.pallas_call(kernel, out_shape=outs, in_specs=[scalars if op.dtype == j...  4.9 us
    ppermute x3, starting transfers between devices, across(): return lax.ppermute(array, ('row', 'col'), pairs)  3.65 us
  transfers between devices with their start and end apart: 22, of which 8 were waited for; matrix products, arithmetic and copies ran while one was open for 0% of the time, Pallas kernels for 4%

profile of v3, /device:TPU:28, one launch (start us, length us, event | category | flops | bytes accessed | tf_op | source)
XLA Modules:
  0.0 80.5 jit_solution(1030811830892906848)
XLA Ops:
  0.0 1.4 %slice_bitcast_fusion = (f32[2,128,512]{2,1,0:T(8,128)S(1)}, f32[2,128,512]{2,1,0:T(8,128)S(1)}) fusion(f32[1,4,128,512]{3,2,1,0:T(8,128)} %param.4), kind=kLoop, calls=%fused_computation | loop fusion | bytes 2097152 | tf_op jit(solution)/shard_map/slice | solution.py:247
  1.4 1.6 %collective-permute-start.3 = (f32[2,128,512]{2,1,0:T(8,128)S(1)}, f32[2,128,512]{2,1,0:T(8,128)S(1)}, u32[]{:S(2)}, u32[]{:S(2)}) collective-permute-start(f32[2,128,512]{2,1,0:T(8,128)S(1)} %get-tuple-element.50), channel_id=1, source_target_pairs={{0,16},{1,17},{2,18},{3,19},{4,20},{5,21},{6,22},{7,23},{8,24},{9,... | collective-permute-start | bytes 1572872 | tf_op jit(solution)/shard_map/ppermute | solution.py:214
  3.0 0.6 collective-permute-start
  3.7 11.4 %collective-permute-done.3.refs_6_ = f32[2,128,512]{2,1,0:T(8,128)S(1)} collective-permute-done((f32[2,128,512]{2,1,0:T(8,128)S(1)}, f32[2,128,512]{2,1,0:T(8,128)S(1)}, u32[]{:S(2)}, u32[]{:S(2)}) %collective-permute-start.3) | collective-permute-done | bytes 524320 | tf_op jit(solution)/shard_map/ppermute | solution.py:214
  15.2 1.6 %collective-permute-start.5 = (f32[1,128,512]{2,1,0:T(8,128)S(1)}, f32[1,128,512]{2,1,0:T(8,128)S(1)}, u32[]{:S(2)}, u32[]{:S(2)}) collective-permute-start(f32[1,128,512]{2,1,0:T(8,128)S(1)} %get-tuple-element.52), channel_id=1, source_target_pairs={{0,16},{1,17},{2,18},{3,19},{4,20},{5,21},{6,22},{7,23},{8,24},{9,... | collective-permute-start | bytes 786440 | tf_op jit(solution)/shard_map/ppermute | solution.py:214
  17.3 1.9 %collective-permute-start.13 = (f32[2,128,512]{2,1,0:T(8,128)S(1)}, f32[2,128,512]{2,1,0:T(8,128)S(1)}, u32[]{:S(2)}, u32[]{:S(2)}) collective-permute-start(f32[2,128,512]{2,1,0:T(8,128)S(1)} %get-tuple-element.49), channel_id=1, source_target_pairs={{0,8},{1,2},{3,11},{4,5},{6,14},{7,15},{8,0},{9,10},{11,3},{12,13}... | collective-permute-start | bytes 1572872 | tf_op jit(solution)/shard_map/ppermute | solution.py:206
  19.2 5.2 %collective-permute-done.5.refs_4_.refs_10_ = f32[1,128,512]{2,1,0:T(8,128)S(1)} collective-permute-done((f32[1,128,512]{2,1,0:T(8,128)S(1)}, f32[1,128,512]{2,1,0:T(8,128)S(1)}, u32[]{:S(2)}, u32[]{:S(2)}) %collective-permute-start.5) | collective-permute-done | bytes 262176 | tf_op jit(solution)/shard_map/ppermute | solution.py:214
  24.4 5.2 %collective-permute-done.8.refs_4_.refs_14_ = f32[1,128,512]{2,1,0:T(8,128)S(1)} collective-permute-done((f32[1,128,512]{2,1,0:T(8,128)S(1)}, f32[1,128,512]{2,1,0:T(8,128)S(1)}, u32[]{:S(2)}, u32[]{:S(2)}) %collective-permute-start.8) | collective-permute-done | bytes 262176 | tf_op jit(solution)/shard_map/ppermute | solution.py:214
  29.6 2.4 %collective-permute-start.17 = (f32[1,128,512]{2,1,0:T(8,128)S(1)}, f32[1,128,512]{2,1,0:T(8,128)S(1)}, u32[]{:S(2)}, u32[]{:S(2)}) collective-permute-start(f32[1,128,512]{2,1,0:T(8,128)S(1)} %collective-permute-done.8.refs_4_.refs_14_), channel_id=1, source_target_pairs={{0,8},{1,2},{3,11},{4,5},{6,14},{7,15},{8,0},{9,10},{11,3},{12,13}... | collective-permute-start | bytes 786440 | tf_op jit(solution)/shard_map/ppermute | solution.py:206
  32.0 1.9 %collective-permute-start.15 = (f32[1,128,512]{2,1,0:T(8,128)S(1)}, f32[1,128,512]{2,1,0:T(8,128)S(1)}, u32[]{:S(2)}, u32[]{:S(2)}) collective-permute-start(f32[1,128,512]{2,1,0:T(8,128)S(1)} %collective-permute-done.5.refs_4_.refs_10_), channel_id=1, source_target_pairs={{0,8},{1,2},{3,11},{4,5},{6,14},{7,15},{8,0},{9,10},{11,3},{12,13}... | collective-permute-start | bytes 786440 | tf_op jit(solution)/shard_map/ppermute | solution.py:206
  33.9 0.9 %shard_map.37 = (f32[128,512]{1,0:T(8,128)S(1)}, f32[128,1024]{1,0:T(8,128)S(1)}, bf16[512,512]{1,0:T(8,128)(2,1)S(1)}, bf16[512,512]{1,0:T(8,128)(2,1)S(1)}, bf...) custom-call(s32[8]{0:T(128)S(1)} %copy-done.2, f32[128,512]{1,0:T(8,128)S(1)} %copy-done.1, ...), custom_call_target="tpu_custom_call" | custom-call | tf_op jit(solution)/shard_map/pallas_call | solution.py:225
  34.8 0.6 shard_map.38
  35.4 0.6 shard_map.39
  36.0 1.5 %collective-permute-start.10 = (f32[128,512]{1,0:T(8,128)S(1)}, f32[128,512]{1,0:T(8,128)S(1)}, u32[]{:S(2)}, u32[]{:S(2)}) collective-permute-start(f32[128,512]{1,0:T(8,128)S(1)} %shard_map.39), channel_id=1, source_target_pairs={{0,1},{1,0},{2,10},{3,4},{4,3},{5,13},{6,7},{7,6},{8,9},{9,8},{10,... | collective-permute-start | bytes 786440 | tf_op jit(solution)/shard_map/ppermute | solution.py:206
  37.5 0.6 collective-permute-start.7
  38.7 6.6 %collective-permute-done.10.refs_2_ = f32[128,512]{1,0:T(8,128)S(1)} collective-permute-done((f32[128,512]{1,0:T(8,128)S(1)}, f32[128,512]{1,0:T(8,128)S(1)}, u32[]{:S(2)}, u32[]{:S(2)}) %collective-permute-start.10) | collective-permute-done | bytes 262176 | tf_op jit(solution)/shard_map/ppermute | solution.py:206
  45.3 9.7 %collective-permute-done.7.refs_1_ = f32[128,512]{1,0:T(8,128)S(1)} collective-permute-done((f32[128,512]{1,0:T(8,128)S(1)}, f32[128,512]{1,0:T(8,128)S(1)}, u32[]{:S(2)}, u32[]{:S(2)}) %collective-permute-start.7) | collective-permute-done | bytes 262176 | tf_op jit(solution)/shard_map/ppermute | solution.py:206
  55.0 1.0 %shard_map.40 = (f32[128,512]{1,0:T(8,128)S(1)}, f32[128,512]{1,0:T(8,128)S(1)}) custom-call(s32[8]{0:T(128)S(1)} %copy-done.2, f32[128,512]{1,0:T(8,128)S(1)} %collective-permute-done.7.refs_1_, f32[128,512]{1,0:T(8,128)S(1)} %collective-permute-done.10.refs_2_, bf16[512,512]{1,0:T(8,128)(2,1)S(1)} %get-tuple-element.31.refs_3_.refs_7_, ...), custom_call_target="tpu_custom_call" | custom-call | tf_op jit(solution)/shard_map/pallas_call | solution.py:225
  56.1 1.3 %collective-permute-start.19 = (f32[128,512]{1,0:T(8,128)S(1)}, f32[128,512]{1,0:T(8,128)S(1)}, u32[]{:S(2)}, u32[]{:S(2)}) collective-permute-start(f32[128,512]{1,0:T(8,128)S(1)} %get-tuple-element.35.own1), channel_id=1, source_target_pairs={{0,8},{1,9},{3,11},{4,2},{6,14},{7,5},{8,0},{9,1},{11,3},{12,10},{... | collective-permute-start | bytes 786440 | tf_op jit(solution)/shard_map/ppermute | solution.py:206
  57.6 0.6 shard_map.42
  58.1 5.7 %collective-permute-done.19.refs_2_ = f32[128,512]{1,0:T(8,128)S(1)} collective-permute-done((f32[128,512]{1,0:T(8,128)S(1)}, f32[128,512]{1,0:T(8,128)S(1)}, u32[]{:S(2)}, u32[]{:S(2)}) %collective-permute-start.19) | collective-permute-done | bytes 262176 | tf_op jit(solution)/shard_map/ppermute | solution.py:206
  64.5 3.4 %collective-permute-start.21 = (f32[128,512]{1,0:T(8,128)S(1)}, f32[128,512]{1,0:T(8,128)S(1)}, u32[]{:S(2)}, u32[]{:S(2)}) collective-permute-start(f32[128,512]{1,0:T(8,128)S(1)} %get-tuple-element.48), channel_id=1, source_target_pairs={{0,8},{1,9},{2,4},{3,11},{4,2},{5,7},{6,14},{7,5},{8,0},{9,1},{10,... | collective-permute-start | bytes 786440 | tf_op jit(solution)/shard_map/ppermute | solution.py:206
  67.8 11.9 %collective-permute-done.21.far = f32[128,512]{1,0:T(8,128)S(1)} collective-permute-done((f32[128,512]{1,0:T(8,128)S(1)}, f32[128,512]{1,0:T(8,128)S(1)}, u32[]{:S(2)}, u32[]{:S(2)}) %collective-permute-start.21) | collective-permute-done | bytes 262176 | tf_op jit(solution)/shard_map/ppermute | solution.py:206
  79.7 0.7 shard_map.44
  (36 shorter events, 2.2 us)
Async XLA Ops:
  0.0 3.0 %copy-start.1 = (f32[128,512]{1,0:T(8,128)S(1)}, f32[128,512]{1,0:T(8,128)}, u32[]{:S(2)}) copy-start(f32[128,512]{1,0:T(8,128)} %refs_1_.1) | copy-start | bytes 786436
  1.4 13.7 %collective-permute-start.3 = (f32[2,128,512]{2,1,0:T(8,128)S(1)}, f32[2,128,512]{2,1,0:T(8,128)S(1)}, u32[]{:S(2)}, u32[]{:S(2)}) collective-permute-start(f32[2,128,512]{2,1,0:T(8,128)S(1)} %get-tuple-element.50), channel_id=1, source_target_pairs={{0,16},{1,17},{2,18},{3,19},{4,20},{5,21},{6,22},{7,23},{8,24},{9,... | collective-permute-start | bytes 1572872 | tf_op jit(solution)/shard_map/ppermute | solution.py:214
  3.0 29.0 %collective-permute-start.2 = (f32[4,128,512]{2,1,0:T(8,128)S(1)}, f32[4,128,512]{2,1,0:T(8,128)S(1)}, u32[]{:S(2)}, u32[]{:S(2)}) collective-permute-start(f32[4,128,512]{2,1,0:T(8,128)S(1)} %bitcast.9), channel_id=1, source_target_pairs={{0,8},{8,0},{16,24},{24,16},{1,9},{9,1},{17,25},{25,17},{2,10},{10... | collective-permute-start | bytes 3145736 | tf_op jit(solution)/shard_map/ppermute | solution.py:219
  3.0 13.8 %collective-permute-start = (f32[128,512]{1,0:T(8,128)S(1)}, f32[128,512]{1,0:T(8,128)S(1)}, u32[]{:S(2)}, u32[]{:S(2)}) collective-permute-start(f32[128,512]{1,0:T(8,128)S(1)} %copy-done.1), channel_id=1, source_target_pairs={{0,1},{1,0},{2,10},{3,4},{4,3},{5,13},{6,7},{7,6},{8,9},{9,8},{10,... | collective-permute-start | bytes 786440 | tf_op jit(solution)/shard_map/ppermute | solution.py:206
  3.5 13.7 %collective-permute-start.1 = (f32[128,512]{1,0:T(8,128)S(1)}, f32[128,512]{1,0:T(8,128)S(1)}, u32[]{:S(2)}, u32[]{:S(2)}) collective-permute-start(f32[128,512]{1,0:T(8,128)S(1)} %copy-done.1), channel_id=1, source_target_pairs={{0,2},{1,9},{2,0},{3,5},{4,12},{5,3},{6,14},{7,15},{8,10},{9,1},{1... | collective-permute-start | bytes 786440 | tf_op jit(solution)/shard_map/ppermute | solution.py:206
  15.1 14.4 %collective-permute-start.4 = (f32[2,128,512]{2,1,0:T(8,128)S(1)}, f32[2,128,512]{2,1,0:T(8,128)S(1)}, u32[]{:S(2)}, u32[]{:S(2)}) collective-permute-start(f32[2,128,512]{2,1,0:T(8,128)S(1)} %collective-permute-done.3.refs_6_), channel_id=1, source_target_pairs={{0,8},{8,0},{16,24},{24,16},{1,9},{9,1},{17,25},{25,17},{2,10},{10... | collective-permute-start | bytes 1572872 | tf_op jit(solution)/shard_map/ppermute | solution.py:219
  15.2 9.2 %collective-permute-start.5 = (f32[1,128,512]{2,1,0:T(8,128)S(1)}, f32[1,128,512]{2,1,0:T(8,128)S(1)}, u32[]{:S(2)}, u32[]{:S(2)}) collective-permute-start(f32[1,128,512]{2,1,0:T(8,128)S(1)} %get-tuple-element.52), channel_id=1, source_target_pairs={{0,16},{1,17},{2,18},{3,19},{4,20},{5,21},{6,22},{7,23},{8,24},{9,... | collective-permute-start | bytes 786440 | tf_op jit(solution)/shard_map/ppermute | solution.py:214
  16.7 17.2 %copy-start.2 = (s32[8]{0:T(128)S(1)}, s32[8]{0:T(128)}, u32[]{:S(2)}) copy-start(s32[8]{0:T(128)} %refs_0_.11) | copy-start | bytes 100
  16.7 12.8 %collective-permute-start.8 = (f32[1,128,512]{2,1,0:T(8,128)S(1)}, f32[1,128,512]{2,1,0:T(8,128)S(1)}, u32[]{:S(2)}, u32[]{:S(2)}) collective-permute-start(f32[1,128,512]{2,1,0:T(8,128)S(1)} %get-tuple-element.51), channel_id=1, source_target_pairs={{0,16},{1,17},{2,18},{3,19},{4,20},{5,21},{6,22},{7,23},{8,24},{9,... | collective-permute-start | bytes 786440 | tf_op jit(solution)/shard_map/ppermute | solution.py:214
  17.3 20.8 %collective-permute-start.13 = (f32[2,128,512]{2,1,0:T(8,128)S(1)}, f32[2,128,512]{2,1,0:T(8,128)S(1)}, u32[]{:S(2)}, u32[]{:S(2)}) collective-permute-start(f32[2,128,512]{2,1,0:T(8,128)S(1)} %get-tuple-element.49), channel_id=1, source_target_pairs={{0,8},{1,2},{3,11},{4,5},{6,14},{7,15},{8,0},{9,10},{11,3},{12,13}... | collective-permute-start | bytes 1572872 | tf_op jit(solution)/shard_map/ppermute | solution.py:206
  24.4 10.4 %collective-permute-start.6 = (f32[1,128,512]{2,1,0:T(8,128)S(1)}, f32[1,128,512]{2,1,0:T(8,128)S(1)}, u32[]{:S(2)}, u32[]{:S(2)}) collective-permute-start(f32[1,128,512]{2,1,0:T(8,128)S(1)} %collective-permute-done.5.refs_4_.refs_10_), channel_id=1, source_target_pairs={{0,8},{8,0},{16,24},{24,16},{1,9},{9,1},{17,25},{25,17},{2,10},{10... | collective-permute-start | bytes 786440 | tf_op jit(solution)/shard_map/ppermute | solution.py:219
  29.6 5.9 %collective-permute-start.9 = (f32[1,128,512]{2,1,0:T(8,128)S(1)}, f32[1,128,512]{2,1,0:T(8,128)S(1)}, u32[]{:S(2)}, u32[]{:S(2)}) collective-permute-start(f32[1,128,512]{2,1,0:T(8,128)S(1)} %collective-permute-done.8.refs_4_.refs_14_), channel_id=1, source_target_pairs={{0,8},{8,0},{16,24},{24,16},{1,9},{9,1},{17,25},{25,17},{2,10},{10... | collective-permute-start | bytes 786440 | tf_op jit(solution)/shard_map/ppermute | solution.py:219
  29.6 8.5 %collective-permute-start.17 = (f32[1,128,512]{2,1,0:T(8,128)S(1)}, f32[1,128,512]{2,1,0:T(8,128)S(1)}, u32[]{:S(2)}, u32[]{:S(2)}) collective-permute-start(f32[1,128,512]{2,1,0:T(8,128)S(1)} %collective-permute-done.8.refs_4_.refs_14_), channel_id=1, source_target_pairs={{0,8},{1,2},{3,11},{4,5},{6,14},{7,15},{8,0},{9,10},{11,3},{12,13}... | collective-permute-start | bytes 786440 | tf_op jit(solution)/shard_map/ppermute | solution.py:206
  32.0 6.6 %collective-permute-start.15 = (f32[1,128,512]{2,1,0:T(8,128)S(1)}, f32[1,128,512]{2,1,0:T(8,128)S(1)}, u32[]{:S(2)}, u32[]{:S(2)}) collective-permute-start(f32[1,128,512]{2,1,0:T(8,128)S(1)} %collective-permute-done.5.refs_4_.refs_10_), channel_id=1, source_target_pairs={{0,8},{1,2},{3,11},{4,5},{6,14},{7,15},{8,0},{9,10},{11,3},{12,13}... | collective-permute-start | bytes 786440 | tf_op jit(solution)/shard_map/ppermute | solution.py:206
  36.0 9.2 %collective-permute-start.10 = (f32[128,512]{1,0:T(8,128)S(1)}, f32[128,512]{1,0:T(8,128)S(1)}, u32[]{:S(2)}, u32[]{:S(2)}) collective-permute-start(f32[128,512]{1,0:T(8,128)S(1)} %shard_map.39), channel_id=1, source_target_pairs={{0,1},{1,0},{2,10},{3,4},{4,3},{5,13},{6,7},{7,6},{8,9},{9,8},{10,... | collective-permute-start | bytes 786440 | tf_op jit(solution)/shard_map/ppermute | solution.py:206
  37.5 17.5 %collective-permute-start.7 = (f32[128,512]{1,0:T(8,128)S(1)}, f32[128,512]{1,0:T(8,128)S(1)}, u32[]{:S(2)}, u32[]{:S(2)}) collective-permute-start(f32[128,512]{1,0:T(8,128)S(1)} %get-tuple-element.29), channel_id=1, source_target_pairs={{0,1},{1,0},{2,10},{3,4},{4,3},{5,13},{6,7},{7,6},{8,9},{9,8},{10,... | collective-permute-start | bytes 786440 | tf_op jit(solution)/shard_map/ppermute | solution.py:206
  38.1 19.3 %collective-permute-start.14 = (f32[2,128,512]{2,1,0:T(8,128)S(1)}, f32[2,128,512]{2,1,0:T(8,128)S(1)}, u32[]{:S(2)}, u32[]{:S(2)}) collective-permute-start(f32[2,128,512]{2,1,0:T(8,128)S(1)} %collective-permute-done.13.refs_0_.refs_4_), channel_id=1, source_target_pairs={{0,8},{8,0},{16,24},{24,16},{1,9},{9,1},{17,25},{25,17},{2,10},{10... | collective-permute-start | bytes 1572872 | tf_op jit(solution)/shard_map/ppermute | solution.py:219
  38.1 17.9 %collective-permute-start.18 = (f32[1,128,512]{2,1,0:T(8,128)S(1)}, f32[1,128,512]{2,1,0:T(8,128)S(1)}, u32[]{:S(2)}, u32[]{:S(2)}) collective-permute-start(f32[1,128,512]{2,1,0:T(8,128)S(1)} %collective-permute-done.17.refs_6_), channel_id=1, source_target_pairs={{0,8},{8,0},{16,24},{24,16},{1,9},{9,1},{17,25},{25,17},{2,10},{10... | collective-permute-start | bytes 786440 | tf_op jit(solution)/shard_map/ppermute | solution.py:219
  38.6 18.7 %collective-permute-start.16 = (f32[1,128,512]{2,1,0:T(8,128)S(1)}, f32[1,128,512]{2,1,0:T(8,128)S(1)}, u32[]{:S(2)}, u32[]{:S(2)}) collective-permute-start(f32[1,128,512]{2,1,0:T(8,128)S(1)} %collective-permute-done.15.refs_2_), channel_id=1, source_target_pairs={{0,8},{8,0},{16,24},{24,16},{1,9},{9,1},{17,25},{25,17},{2,10},{10... | collective-permute-start | bytes 786440 | tf_op jit(solution)/shard_map/ppermute | solution.py:219
  45.3 12.2 %collective-permute-start.12 = (f32[128,512]{1,0:T(8,128)S(1)}, f32[128,512]{1,0:T(8,128)S(1)}, u32[]{:S(2)}, u32[]{:S(2)}) collective-permute-start(f32[128,512]{1,0:T(8,128)S(1)} %get-tuple-element.27.own0), channel_id=1, source_target_pairs={{0,8},{1,9},{2,3},{3,2},{4,12},{5,6},{6,5},{7,15},{8,0},{9,1},{10,... | collective-permute-start | bytes 786440 | tf_op jit(solution)/shard_map/ppermute | solution.py:206
  56.0 1.6 %collective-permute-start.11 = (f32[128,512]{1,0:T(8,128)S(1)}, f32[128,512]{1,0:T(8,128)S(1)}, u32[]{:S(2)}, u32[]{:S(2)}) collective-permute-start(f32[128,512]{1,0:T(8,128)S(1)} %get-tuple-element.36), channel_id=1, source_target_pairs={{0,1},{1,2},{2,0},{3,4},{4,5},{5,3},{6,14},{7,15},{8,9},{9,10},{10... | collective-permute-start | bytes 786440 | tf_op jit(solution)/shard_map/ppermute | solution.py:206
  56.1 7.8 %collective-permute-start.19 = (f32[128,512]{1,0:T(8,128)S(1)}, f32[128,512]{1,0:T(8,128)S(1)}, u32[]{:S(2)}, u32[]{:S(2)}) collective-permute-start(f32[128,512]{1,0:T(8,128)S(1)} %get-tuple-element.35.own1), channel_id=1, source_target_pairs={{0,8},{1,9},{3,11},{4,2},{6,14},{7,5},{8,0},{9,1},{11,3},{12,10},{... | collective-permute-start | bytes 786440 | tf_op jit(solution)/shard_map/ppermute | solution.py:206
  64.4 3.4 %collective-permute-start.20 = (f32[128,512]{1,0:T(8,128)S(1)}, f32[128,512]{1,0:T(8,128)S(1)}, u32[]{:S(2)}, u32[]{:S(2)}) collective-permute-start(f32[128,512]{1,0:T(8,128)S(1)} %get-tuple-element.47), channel_id=1, source_target_pairs={{0,8},{1,9},{2,3},{3,2},{4,12},{5,6},{6,5},{7,15},{8,0},{9,1},{10,... | collective-permute-start | bytes 786440 | tf_op jit(solution)/shard_map/ppermute | solution.py:206
  64.5 15.3 %collective-permute-start.21 = (f32[128,512]{1,0:T(8,128)S(1)}, f32[128,512]{1,0:T(8,128)S(1)}, u32[]{:S(2)}, u32[]{:S(2)}) collective-permute-start(f32[128,512]{1,0:T(8,128)S(1)} %get-tuple-element.48), channel_id=1, source_target_pairs={{0,8},{1,9},{2,4},{3,11},{4,2},{5,7},{6,14},{7,5},{8,0},{9,1},{10,... | collective-permute-start | bytes 786440 | tf_op jit(solution)/shard_map/ppermute | solution.py:206
  (1 other events, 3.0 us)
